TPU v7x, 256 devices: a whole 4x4x8 slice. The times are simulated.
256 devices in a mesh: dp: 8 (over y, core), row: 16 (over x_hi, z), view: 2 (over x_lo).
Axes of the slice: x: 4 (x_hi: 2, x_lo: 2; x = x_hi * 2 + x_lo), y: 4, z: 8, core: 2. Of those that a mesh axis runs over, the one named last changes fastest.
Arguments:
- frames_in: float32 [2, 8, 64, 64, 480], P('view', 'dp', None, 'row'), may hold values from -13 to 13
- cotangent: float32 [2, 8, 64, 64, 480], P('view', 'dp', None, 'row'), may hold values from -36 to 36
- expand_in: float32 [128, 64], replicated, may hold values from -0.75 to 0.75
- conv_kernel: float32 [128, 3, 3], replicated, may hold values from -2 to 2
- pool_proj: float32 [64, 64], replicated, may hold values from -1.5 to 1.5
- pool_bias: float32 [64], replicated, may hold values from 0.5 to 1.5
- squeeze_out: float32 [64, 64], replicated, may hold values from -0.75 to 0.75
- branch_scale: float32 [64], replicated, may hold values from 0.3 to 1
- ffn_expand: float32 [128, 64], replicated, may hold values from -0.75 to 0.75
- ffn_shrink: float32 [64, 64], replicated, may hold values from -0.75 to 0.75
- ffn_scale: float32 [64], replicated, may hold values from 0.3 to 1
- query_proj: float32 [2, 64, 64], P('view'), may hold values from -1.5 to 1.5
- value_proj: float32 [2, 64, 64], P('view'), may hold values from -0.75 to 0.75
- cross_scale: float32 [2, 64], P('view'), may hold values from 0.3 to 1
Outputs:
- block_out: float32 [2, 8, 64, 64, 480], P('view', 'dp', None, 'row')
- grad_in: float32 [2, 8, 64, 64, 480], P('view', 'dp', None, 'row')
- grad_expand: float32 [128, 64], replicated
- grad_kernel: float32 [128, 3, 3], replicated
- grad_pool: float32 [64, 64], replicated
- grad_bias: float32 [64], replicated
- grad_squeeze: float32 [64, 64], replicated
- grad_branch: float32 [64], replicated
- grad_ffn_up: float32 [128, 64], replicated
- grad_ffn_down: float32 [64, 64], replicated
- grad_ffn_scale: float32 [64], replicated
- grad_query: float32 [2, 64, 64], P('view')
- grad_value: float32 [2, 64, 64], P('view')
- grad_cross: float32 [2, 64], P('view')
All inputs are finite; a program needn't handle non-finite values.
Results may differ from a plain program's by a relative error of at most 0.0003.
Values sent between devices are 32-bit elements; how exact they have to be, the bound alone decides.
A program may use at most 64 MiB of HBM per device.

v0:
```python
import functools

import jax
import jax.numpy as jnp
from jax import lax
from jax.experimental import pallas as pl
from jax.experimental.pallas import tpu as pltpu
from jax.sharding import PartitionSpec as P

epsilon = 1e-06
WIDE = 512
f32 = jnp.float32
bf16 = jnp.bfloat16
MESH = pl.DeviceIdType.MESH


def halves(x):
    high = x.astype(bf16)
    return high, (x - high.astype(f32)).astype(bf16)


def left_parts(x):
    high, low = halves(x)
    return jnp.concatenate([high, low, high], axis=0)


def right_parts(x):
    high, low = halves(x)
    return jnp.concatenate([high, high, low], axis=0)


def dot_nn(a, b):
    return lax.dot_general(a, b, (((1,), (0,)), ((), ())), preferred_element_type=f32)


def dot_nt(a, b):
    return lax.dot_general(a, b, (((1,), (1,)), ((), ())), preferred_element_type=f32)


def dot_tn(a, b):
    return lax.dot_general(a, b, (((0,), (0,)), ((), ())), preferred_element_type=f32)


def over_pixels(a, b):
    a_high, a_low = halves(a)
    b_high, b_low = halves(b)
    return dot_nt(
        jnp.concatenate([a_high, a_low, a_high], axis=1),
        jnp.concatenate([b_high, b_high, b_low], axis=1),
    )


def fold(x):
    return x[:, :128] + x[:, 128:256] + x[:, 256:384] + x[:, 384:]


def normed(x):
    center = x - jnp.mean(x, axis=0, keepdims=True)
    scale = 1.0 / jnp.sqrt(jnp.mean(center * center, axis=0, keepdims=True) + epsilon)
    return center * scale, scale


def normed_back(grad, value, scale):
    return scale * (
        grad
        - jnp.mean(grad, axis=0, keepdims=True)
        - value * jnp.mean(grad * value, axis=0, keepdims=True)
    )


def block_kernel(
    sizes,
    factor,
    area,
    cols,
    x_ref,
    up_ref,
    expand_ref,
    taps_ref,
    pool_ref,
    bias_ref,
    squeeze_ref,
    branch_ref,
    ffn_up_ref,
    ffn_down_ref,
    ffn_scale_ref,
    query_ref,
    value_ref,
    cross_ref,
    out_ref,
    grad_ref,
    sum_ref,
    x_s,
    c_s,
    cp_s,
    n0_s,
    s0_s,
    d_s,
    cv_s,
    g_s,
    t_s,
    n1_s,
    s1_s,
    e_s,
    u_s,
    h_s,
    hp_s,
    dh_s,
    dhp_s,
    op_s,
    dg_s,
    dr_s,
    dcv_s,
    e_att,
    taps_s,
    fold_s,
    tap_acc,
    queryp_s,
    valuep_s,
    crossp_s,
    pool_s,
    poolg_s,
    part_s,
    first,
    second,
    third,
    expand_f,
    expand_b,
    squeeze_f,
    squeeze_b,
    up_f,
    up_b,
    down_f,
    down_b,
    sends,
    recvs,
    group_sends,
    group_recvs,
):
    rows, lanes = sizes
    row = lax.axis_index("row")
    view = lax.axis_index("view")
    lane = lax.axis_index("dp") * 2 + view
    mine = 2 * view
    theirs = 2 - mine

    def in_row(step):
        return {"row": lax.rem(row + step, rows)}

    def in_lane(step):
        other = lax.rem(lane + step, lanes)
        return {"dp": other // 2, "view": lax.rem(other, 2)}

    above = in_row(rows - 1)
    below = in_row(1)
    partner = {"view": 1 - view}

    barrier = pltpu.get_barrier_semaphore()
    for step in range(1, rows):
        pl.semaphore_signal(barrier, inc=1, device_id=in_row(step), device_id_type=MESH)
    for step in range(1, lanes):
        pl.semaphore_signal(barrier, inc=1, device_id=in_lane(step), device_id_type=MESH)

    def send(index, source, target, device):
        copy = pltpu.make_async_remote_copy(
            src_ref=source,
            dst_ref=target,
            send_sem=sends.at[index],
            recv_sem=recvs.at[index],
            device_id=device,
            device_id_type=MESH,
        )
        copy.start()
        return copy

    def spread(phase, source, target, device, count):
        copies = []
        for step in range(1, count):
            copy = pltpu.make_async_remote_copy(
                src_ref=source(step),
                dst_ref=target,
                send_sem=group_sends.at[phase, step - 1],
                recv_sem=group_recvs.at[phase, step - 1],
                device_id=device(step),
                device_id_type=MESH,
            )
            copy.start()
            copies.append(copy)
        return copies

    for h in range(4):
        x_s[h + 1, :, 384:] = jnp.zeros((64, 128), f32)
        c_s[h, :, 384:] = jnp.zeros((64, 128), f32)
        x_s[h + 1, :, :cols] = x_ref[:, h, :]
        c_s[h, :, :cols] = up_ref[:, h, :]

    pl.semaphore_wait(barrier, rows + lanes - 2)
    halo_up = send(0, x_s.at[1], x_s.at[5], above)
    halo_down = send(1, x_s.at[4], x_s.at[0], below)
    weights_sent = [
        send(2, query_ref, queryp_s, partner),
        send(3, value_ref, valuep_s, partner),
        send(4, cross_ref, crossp_s, partner),
    ]
    cotangent_sent = send(5, c_s.at[pl.ds(theirs, 2)], cp_s, partner)

    def prepare(weight, forward, backward):
        if forward is not None:
            forward[...] = left_parts(weight.T).astype(f32).T.astype(bf16)
        if backward is not None:
            backward[...] = left_parts(weight).astype(f32).T.astype(bf16)

    prepare(expand_ref[...], expand_f, expand_b)
    prepare(squeeze_ref[...], squeeze_f, squeeze_b)
    prepare(ffn_up_ref[...], up_f, up_b)
    prepare(ffn_down_ref[...], down_f, down_b)
    eye = lax.broadcasted_iota(jnp.int32, (64, 128), 0) == lax.broadcasted_iota(
        jnp.int32, (64, 128), 1
    )

    def to_column(vector):
        spread_out = jnp.broadcast_to(vector, (64, vector.shape[1]))
        return jnp.sum(
            jnp.where(eye[:, : vector.shape[1]], spread_out, 0.0), axis=1, keepdims=True
        )

    def to_row(column):
        return jnp.sum(
            jnp.where(eye, jnp.broadcast_to(column, (64, 128)), 0.0), axis=0, keepdims=True
        )

    for tap in range(9):
        taps_s[tap] = jnp.broadcast_to(taps_ref[:, tap : tap + 1], (128, 128))
    bias = to_column(bias_ref[...])
    branch = to_column(branch_ref[...])
    ffn_scale = to_column(ffn_scale_ref[...])
    cross = to_column(cross_ref[...])
    inside = lax.broadcasted_iota(jnp.int32, (1, WIDE), 1) < cols
    part_s[...] = jnp.zeros_like(part_s)
    fold_s[...] = jnp.zeros_like(fold_s)
    tap_acc[...] = jnp.zeros_like(tap_acc)

    def expand_row(h):
        value, scale = normed(x_s[h])
        d_s[h] = dot_nn(expand_f[...], right_parts(value))
        return value, scale

    @pl.loop(1, 5)
    def _(h):
        value, scale = expand_row(h)
        n0_s[h - 1] = value
        s0_s[h - 1] = scale

    halo_up.wait()
    halo_down.wait()

    @pl.when(row == 0)
    def _():
        x_s[0] = jnp.zeros((64, WIDE), f32)

    @pl.when(row == rows - 1)
    def _():
        x_s[5] = jnp.zeros((64, WIDE), f32)

    expand_row(0)
    expand_row(5)

    def tap_at(tap, start, size):
        piece = taps_s[tap, pl.ds(start, size), :]
        return jnp.concatenate([piece] * 4, axis=1)

    @pl.loop(1, 5)
    def _(h):
        for start in range(0, 128, 16):
            columns = [jnp.zeros((16, WIDE), f32)] * 3
            for i in range(3):
                value = d_s[h + i - 1, start : start + 16, :]
                for j in range(3):
                    columns[j] = columns[j] + tap_at(3 * i + j, start, 16) * value
            total = columns[1] + pltpu.roll(columns[0], 1, 1) + pltpu.roll(columns[2], WIDE - 1, 1)
            cv_s[h, start : start + 16, :] = jnp.where(inside, total, 0.0)
        gate = cv_s[h, :64, :] * cv_s[h, 64:, :]
        g_s[h - 1] = gate
        fold_s[0] += fold(gate)

    pool_s[row] = to_row(jnp.sum(fold_s[0], axis=1, keepdims=True))
    copies = spread(0, lambda step: pool_s.at[row], pool_s.at[row], in_row, rows)
    conv_up = send(6, cv_s.at[1], cv_s.at[5], above)
    conv_down = send(7, cv_s.at[4], cv_s.at[0], below)
    for copy in copies:
        copy.wait()
    pooled = jnp.sum(pool_s[...], axis=0) / area
    attention = jnp.sum(pool_ref[...] * pooled[:, :64], axis=1, keepdims=True) + bias

    def tail_row(h):
        squeezed = dot_nn(squeeze_f[...], right_parts(g_s[h] * attention))
        t_s[h] = squeezed
        residual = x_s[h + 1] + branch * squeezed
        value, scale = normed(residual)
        n1_s[h] = value
        s1_s[h] = scale
        expanded = dot_nn(up_f[...], right_parts(value))
        e_s[h] = expanded
        shrunk = dot_nn(down_f[...], right_parts(expanded[:64] * expanded[64:]))
        u_s[h] = shrunk
        h_s[h] = residual + ffn_scale * shrunk

    @pl.loop(0, 2)
    def _(k):
        tail_row(theirs + k)

    hidden_sent = send(8, h_s.at[pl.ds(theirs, 2)], hp_s, partner)

    @pl.loop(0, 2)
    def _(k):
        tail_row(mine + k)

    for copy in weights_sent:
        copy.wait()
    cotangent_sent.wait()
    hidden_sent.wait()
    crossp = to_column(crossp_s[...])

    def query_parts(weight):
        return left_parts(weight.T), left_parts(weight)

    sixteen = lax.broadcasted_iota(jnp.int32, (16, WIDE), 0)
    outside16 = lax.broadcasted_iota(jnp.int32, (16, WIDE), 1) >= cols
    ones16 = jnp.ones((16, WIDE), bf16)
    mask_left = jnp.where(
        sixteen == 0, jnp.where(outside16, -256.0, 0.0), jnp.where(sixteen == 1, 1.0, 0.0)
    ).astype(bf16)
    mask_right = jnp.where(
        sixteen == 0, 1.0, jnp.where((sixteen == 1) & outside16, -256.0, 0.0)
    ).astype(bf16)

    def attend_row(k):
        h = mine + k
        own, other = h_s[h], hp_s[k]
        own_up, other_up = c_s[h], cp_s[k]
        own_n, own_scale = normed(own)
        other_n, other_scale = normed(other)
        own_wq, own_wq_back = query_parts(query_ref[...])
        own_wv, own_wv_back = query_parts(value_ref[...])
        other_wq, other_wq_back = query_parts(queryp_s[...])
        other_wv, other_wv_back = query_parts(valuep_s[...])
        own_q = dot_tn(own_wq, right_parts(own_n))
        other_q = dot_tn(other_wq, right_parts(other_n))
        own_v = dot_tn(own_wv, right_parts(own))
        other_v = dot_tn(other_wv, right_parts(other))
        scores = dot_tn(
            jnp.concatenate([left_parts(own_q * 0.125), mask_left], axis=0),
            jnp.concatenate([right_parts(other_q), mask_right], axis=0),
        )
        weights = jnp.exp(scores)
        e_att[...] = weights
        w_high, w_low = halves(weights)

        def weighted(dot, values):
            high, low = halves(values)
            large = dot(jnp.concatenate([high, ones16, low], axis=0), w_high)
            small = dot(jnp.concatenate([high, ones16], axis=0), w_low)
            bottom = jnp.where(inside, large[64:65] + small[64:65], 1.0)
            return large[:64] + large[80:] + small[:64], 1.0 / bottom

        def through(dot, values, high_m, low_m):
            high, low = halves(values)
            large = dot(jnp.concatenate([high, low], axis=0), high_m)
            return large[:64] + large[64:] + dot(high, low_m)

        own_c, own_r = weighted(dot_nt, other_v)
        other_c, other_r = weighted(dot_nn, own_v)
        own_c = own_c * own_r
        other_c = other_c * other_r
        out_ref[h] = own + cross * own_c
        op_s[k] = other + crossp * other_c
        own_d = cross * own_up * own_r
        other_d = crossp * other_up * other_r
        fold_s[4] += fold(own_up * own_c)
        fold_s[5] += fold(other_up * other_c)
        own_delta, own_delta_low = halves(-jnp.sum(own_d * own_c, axis=0, keepdims=True))
        other_delta, other_delta_low = halves(-jnp.sum(other_d * other_c, axis=0, keepdims=True))
        left_tail = jnp.where(
            sixteen == 0,
            own_delta.astype(f32),
            jnp.where(
                sixteen == 1, own_delta_low.astype(f32), jnp.where(sixteen < 4, 1.0, 0.0)
            ),
        ).astype(bf16)
        right_tail = jnp.where(
            sixteen == 2,
            other_delta.astype(f32),
            jnp.where(
                sixteen == 3, other_delta_low.astype(f32), jnp.where(sixteen < 2, 1.0, 0.0)
            ),
        ).astype(bf16)
        change = dot_tn(
            jnp.concatenate(
                [left_parts(jnp.concatenate([own_d, own_v], axis=0)), left_tail], axis=0
            ),
            jnp.concatenate(
                [right_parts(jnp.concatenate([other_v, other_d], axis=0)), right_tail], axis=0
            ),
        )
        ds_high, ds_low = halves(e_att[...] * change * 0.125)
        other_dv = through(dot_nn, own_d, w_high, w_low)
        own_dv = through(dot_nt, other_d, w_high, w_low)
        other_dq = through(dot_nn, own_q, ds_high, ds_low)
        own_dq = through(dot_nt, other_q, ds_high, ds_low)

        def back(up, dq, dv, wq_back, wv_back, value, scale):
            dn = dot_tn(wq_back, right_parts(dq))
            return up + dot_tn(wv_back, right_parts(dv)) + normed_back(dn, value, scale)

        dhp_s[k] = back(
            other_up, other_dq, other_dv, other_wq_back, other_wv_back, other_n, other_scale
        )
        dh_s[h] = back(own_up, own_dq, own_dv, own_wq_back, own_wv_back, own_n, own_scale)
        grads = [
            over_pixels(own_dq, own_n),
            over_pixels(other_dq, other_n),
            over_pixels(own_dv, own),
            over_pixels(other_dv, other),
        ]
        for start, (first_grad, second_grad) in ((256, grads[:2]), (320, grads[2:])):
            part_s[start : start + 64, :64] += jnp.where(view == 0, first_grad, second_grad)
            part_s[start : start + 64, 64:] += jnp.where(view == 0, second_grad, first_grad)

    returned = []
    for k in range(2):
        attend_row(k)
        returned.append(send(9 + k, dhp_s.at[k], dh_s.at[mine + k], partner))
    out_sent = send(11, op_s, out_ref.at[pl.ds(mine, 2)], partner)

    def tail_back_row(h):
        up = dh_s[h]
        fold_s[1] += fold(up * u_s[h])
        du = ffn_scale * up
        expanded = e_s[h]
        gate = expanded[:64] * expanded[64:]
        dgate = dot_nn(down_b[...], right_parts(du))
        part_s[128:192, 64:] += over_pixels(du, gate)
        de = jnp.concatenate([dgate * expanded[64:], dgate * expanded[:64]], axis=0)
        part_s[:128, 64:] += over_pixels(de, n1_s[h])
        dn = dot_nn(up_b[...], right_parts(de))
        dr = up + normed_back(dn, n1_s[h], s1_s[h])
        dr_s[h] = dr
        fold_s[2] += fold(dr * t_s[h])
        dt = branch * dr
        g = g_s[h]
        dscaled = dot_nn(squeeze_b[...], right_parts(dt))
        part_s[128:192, :64] += over_pixels(dt, g * attention)
        fold_s[3] += fold(dscaled * g)
        dg_s[h + 1] = dscaled * attention

    @pl.loop(0, 2)
    def _(k):
        tail_back_row(mine + k)

    for copy in returned:
        copy.wait()

    @pl.loop(0, 2)
    def _(k):
        tail_back_row(theirs + k)

    d_attention = jnp.sum(fold_s[3], axis=1, keepdims=True)
    poolg_s[row, :, :64] = jnp.sum(pool_ref[...] * d_attention, axis=0, keepdims=True)
    poolg_s[row, :, 64:] = jnp.zeros((1, 64), f32)
    copies = spread(1, lambda step: poolg_s.at[row], poolg_s.at[row], in_row, rows)
    gate_up = send(12, dg_s.at[1], dg_s.at[5], above)
    gate_down = send(13, dg_s.at[4], dg_s.at[0], below)
    conv_up.wait()
    conv_down.wait()
    for copy in copies:
        copy.wait()
    constant = to_column(jnp.sum(poolg_s[...], axis=0) / area)
    gate_up.wait()
    gate_down.wait()

    @pl.loop(0, 6)
    def _(h):
        total = dg_s[h] + constant
        dcv_s[h, :64, :] = total * cv_s[h, 64:, :]
        dcv_s[h, 64:, :] = total * cv_s[h, :64, :]

    @pl.when(row == 0)
    def _():
        dcv_s[0] = jnp.zeros((128, WIDE), f32)

    @pl.when(row == rows - 1)
    def _():
        dcv_s[5] = jnp.zeros((128, WIDE), f32)

    @pl.loop(0, 8)
    def _(chunk):
        start = pl.multiple_of(chunk * 16, 16)
        size = 16
        for h in range(1, 5):
            center = dcv_s[h, pl.ds(start, size), :]
            moved = [pltpu.roll(center, WIDE - 1, 1), center, pltpu.roll(center, 1, 1)]
            for i in range(3):
                value = d_s[h + i - 1, pl.ds(start, size), :]
                for j in range(3):
                    tap_acc[3 * i + j, pl.ds(start, size), :] += fold(moved[j] * value)
        for h in range(1, 5):
            columns = [jnp.zeros((size, WIDE), f32)] * 3
            for i in range(3):
                value = dcv_s[h - i + 1, pl.ds(start, size), :]
                for j in range(3):
                    columns[j] = columns[j] + tap_at(3 * i + j, start, size) * value
            cv_s[h, pl.ds(start, size), :] = (
                columns[1] + pltpu.roll(columns[2], 1, 1) + pltpu.roll(columns[0], WIDE - 1, 1)
            )

    @pl.loop(0, 4)
    def _(h):
        dd = cv_s[h + 1]
        dn = dot_nn(expand_b[...], right_parts(dd))
        part_s[:128, :64] += over_pixels(dd, n0_s[h])
        grad_ref[h] = dr_s[h] + normed_back(dn, n0_s[h], s0_s[h])

    place = lax.broadcasted_iota(jnp.int32, (64, 128), 1)
    mixed = d_attention * pooled

    def columns_of(value):
        return jnp.sum(value, axis=1, keepdims=True)

    items = []
    for tap in range(9):
        items.append(columns_of(tap_acc[tap, :64, :]))
    for tap in range(9):
        items.append(columns_of(tap_acc[tap, 64:, :]))
    items += [d_attention, columns_of(fold_s[2]), columns_of(fold_s[1])]
    own_cross = columns_of(fold_s[4])
    other_cross = columns_of(fold_s[5])
    items.append(jnp.where(view == 0, own_cross, other_cross))
    items.append(jnp.where(view == 0, other_cross, own_cross))
    for index, item in enumerate(items):
        mixed = jnp.where(place == 64 + index, item, mixed)
    part_s[192:256, :] = mixed

    size = 384 // rows

    def chunk_at(index):
        return part_s.at[pl.ds(pl.multiple_of(index * size, 8), size)]

    copies = spread(
        2, lambda step: chunk_at(lax.rem(row + step, rows)), first.at[row], in_row, rows
    )
    first[row] = part_s[pl.ds(pl.multiple_of(row * size, 8), size), :]
    for copy in copies:
        copy.wait()
    second[lane] = jnp.sum(first[...], axis=0)
    copies = spread(3, lambda step: second.at[lane], second.at[lane], in_lane, lanes)
    for copy in copies:
        copy.wait()
    third[row] = jnp.sum(second[...], axis=0) * factor
    copies = spread(4, lambda step: third.at[row], third.at[row], in_row, rows)
    for copy in copies:
        copy.wait()
    sum_ref[...] = third[...]
    out_sent.wait()


def per_device(rows, lanes, *arrays):
    (
        frames_in,
        cotangent,
        expand_in,
        conv_kernel,
        pool_proj,
        pool_bias,
        squeeze_out,
        branch_scale,
        ffn_expand,
        ffn_shrink,
        ffn_scale,
        query_proj,
        value_proj,
        cross_scale,
    ) = arrays
    cols = frames_in.shape[4]
    area = 4 * rows * cols
    factor = (lanes * area) ** (-0.5)
    wide = functools.partial(jax.ShapeDtypeStruct, dtype=f32)

    def fields(*shape):
        return pltpu.VMEM(shape, f32)

    size = 384 // rows
    scratch = [
        fields(6, 64, WIDE),
        fields(4, 64, WIDE),
        fields(2, 64, WIDE),
        fields(4, 64, WIDE),
        fields(4, 1, WIDE),
        fields(6, 128, WIDE),
        fields(6, 128, WIDE),
        fields(4, 64, WIDE),
        fields(4, 64, WIDE),
        fields(4, 64, WIDE),
        fields(4, 1, WIDE),
        fields(4, 128, WIDE),
        fields(4, 64, WIDE),
        fields(4, 64, WIDE),
        fields(2, 64, WIDE),
        fields(4, 64, WIDE),
        fields(2, 64, WIDE),
        fields(2, 64, WIDE),
        fields(6, 64, WIDE),
        fields(4, 64, WIDE),
        fields(6, 128, WIDE),
        fields(WIDE, WIDE),
        fields(9, 128, 128),
        fields(6, 64, 128),
        fields(9, 128, 128),
        fields(64, 64),
        fields(64, 64),
        fields(1, 64),
        fields(rows, 1, 128),
        fields(rows, 1, 128),
        fields(384, 128),
        fields(rows, size, 128),
        fields(lanes, size, 128),
        fields(rows, size, 128),
        pltpu.VMEM((128, 192), bf16),
        pltpu.VMEM((64, 384), bf16),
        pltpu.VMEM((64, 192), bf16),
        pltpu.VMEM((64, 192), bf16),
        pltpu.VMEM((128, 192), bf16),
        pltpu.VMEM((64, 384), bf16),
        pltpu.VMEM((64, 192), bf16),
        pltpu.VMEM((64, 192), bf16),
        pltpu.SemaphoreType.DMA((14,)),
        pltpu.SemaphoreType.DMA((14,)),
        pltpu.SemaphoreType.DMA((5, 15)),
        pltpu.SemaphoreType.DMA((5, 15)),
    ]
    out, grad, total = pl.pallas_call(
        functools.partial(block_kernel, (rows, lanes), factor, area, cols),
        out_shape=(wide((4, 64, WIDE)), wide((4, 64, WIDE)), wide((rows, size, 128))),
        in_specs=[pl.BlockSpec(memory_space=pltpu.VMEM)] * 14,
        out_specs=(pl.BlockSpec(memory_space=pltpu.VMEM),) * 3,
        scratch_shapes=scratch,
        compiler_params=pltpu.CompilerParams(
            collective_id=0, has_side_effects=True, vmem_limit_bytes=56 * 2**20
        ),
    )(
        frames_in[0, 0],
        cotangent[0, 0],
        expand_in,
        conv_kernel.reshape(128, 9),
        pool_proj,
        pool_bias[None],
        squeeze_out,
        branch_scale[None],
        ffn_expand,
        ffn_shrink,
        ffn_scale[None],
        query_proj[0],
        value_proj[0],
        cross_scale,
    )

    def placed(value):
        return value[:, :, :cols].transpose(1, 0, 2)[None, None]

    total = total.reshape(384, 128)
    slot = lax.axis_index("view")
    mixed = total[192:256]
    per_view = total[256:384].reshape(2, 64, 2, 64)
    chosen = lax.dynamic_index_in_dim(per_view, slot, 2, keepdims=False)
    cross = lax.dynamic_index_in_dim(mixed[:, 85:87], slot, 1, keepdims=False)
    return (
        placed(out),
        placed(grad),
        total[:128, :64],
        jnp.concatenate([mixed[:, 64:73], mixed[:, 73:82]], axis=0).reshape(128, 3, 3),
        mixed[:, :64],
        mixed[:, 82],
        total[128:192, :64],
        mixed[:, 83],
        total[:128, 64:],
        total[128:192, 64:],
        mixed[:, 84],
        chosen[0][None],
        chosen[1][None],
        cross[None],
    )


def solution(mesh):
    field = P("view", "dp", None, "row", None)
    copied = (P(),) * 9
    owned = (P("view", None, None), P("view", None, None), P("view", None))
    return jax.shard_map(
        functools.partial(per_device, mesh.shape["row"], 2 * mesh.shape["dp"]),
        mesh=mesh,
        in_specs=(field, field) + copied + owned,
        out_specs=(field, field) + copied + owned,
        check_vma=False,
    )
```

profile of v0, /device:TPU:1, one launch (start us, length us, event | category | flops | bytes accessed | tf_op | source)
XLA Modules:
  0.0 94.7 jit_solution(2128002894720392)
XLA Ops:
  0.6 0.0 copy-start.2
  0.7 1.5 %copy.43.expand_ref = f32[128,64]{1,0:T(8,128)} copy(f32[128,64]{0,1:T(8,128)} %param.16) | data formatting | bytes 65536 | tf_op args[2]
  2.1 0.0 copy-done.2
  2.2 0.0 copy-start.1
  2.2 0.7 copy.44.taps_ref
  2.9 0.0 copy-done.1
  2.9 0.7 copy.45.ffn_up_ref
  3.6 82.0 %shard_map.245 = (f32[4,64,512]{2,1,0:T(8,128)}, f32[4,64,512]{2,1,0:T(8,128)}, f32[16,24,128]{2,1,0:T(8,128)}) custom-call(f32[64,4,480]{2,1,0:T(4,128)} %bitcast.29, f32[64,4,480]{2,1,0:T(4,128)} %bitcast.30, f32[128,64]{1,0:T(8,128)} %copy.43.expand_ref, f32[128,9]{1,0:T(8,128)} %copy.44.taps_ref, f32[64,64]{1,0:T(8,128)} %pool_ref.1, f32[1,64]{1,0:T(1,128)} %bitcast.35, ...), custom_call_target="tpu_custom_call" | custom-call | tf_op jit(solution)/shard_map/pallas_call | solution.py:640
  85.7 1.3 %slice_bitcast_fusion = (f32[1,1,64,4,480]{4,2,3,1,0:T(8,128)S(1)}, f32[1,1,64,4,480]{4,2,3,1,0:T(8,128)S(1)}) fusion(f32[4,64,512]{2,1,0:T(8,128)} %get-tuple-element.18, f32[4,64,512]{2,1,0:T(8,128)} %get-tuple-element.17), kind=kLoop, calls=%fused_computation | loop fusion | bytes 1966080 | tf_op jit(solution)/shard_map/broadcast_in_dim | solution.py:667
  86.9 1.1 %copy.48 = f32[1,1,64,4,480]{4,3,2,1,0:T(4,128)} copy(f32[1,1,64,4,480]{4,2,3,1,0:T(8,128)S(1)} %get-tuple-element.75) | data formatting | bytes 983040
  88.1 0.0 copy-start
  88.1 1.1 %copy.49 = f32[1,1,64,4,480]{4,3,2,1,0:T(4,128)} copy(f32[1,1,64,4,480]{4,2,3,1,0:T(8,128)S(1)} %get-tuple-element.74) | data formatting | bytes 983040
  89.2 0.0 copy-done
  89.2 0.1 fusion.1
  89.3 0.7 copy.50
  90.0 0.1 fusion.2
  90.1 0.1 copy.53
  90.2 0.1 copy.52
  90.2 0.1 pad_maximum_fusion
  90.3 0.6 reshape.45
  90.9 0.7 fusion
  91.6 0.7 slice_reduce_fusion
  92.4 0.7 copy.51
  93.1 0.1 reshape.46
  93.2 0.7 constant_dynamic-slice_fusion.1
  93.9 0.1 slice.91
  94.0 0.7 dynamic-slice_reduce_fusion
  (2 shorter events, 0.0 us)
Async XLA Ops:
  0.6 1.5 %copy-start.2 = (f32[128,3,3]{0,2,1:T(4,128)S(1)}, f32[128,3,3]{0,2,1:T(4,128)}, u32[]{:S(2)}) copy-start(f32[128,3,3]{0,2,1:T(4,128)} %param.17) | copy-start | bytes 13828
  2.2 0.8 copy-start.1
  88.1 1.1 %copy-start = (f32[16,24,128]{2,1,0:T(8,128)S(1)}, f32[16,24,128]{2,1,0:T(8,128)}, u32[]{:S(2)}) copy-start(f32[16,24,128]{2,1,0:T(8,128)} %get-tuple-element.19) | copy-start | bytes 589828
where the time goes:
time: 95.3 us; the launch traced here: 94.7 us
  Pallas kernels  82 us (86%)
  local copies, waits for them, and re-layouts  11.9 us (12%)
    pallas_call x1, Pallas kernels, per_device(): pl.pallas_call(functools.partial(block_kernel, (rows, lanes), factor, are...  82 us
    unnamed x14, local copies, waits for them, and re-layouts  6.05 us

commit v1 on v0

v1 whole, which is shorter than its diff:
```python
import functools

import jax
import jax.numpy as jnp
from jax import lax
from jax.experimental import pallas as pl
from jax.experimental.pallas import tpu as pltpu
from jax.sharding import PartitionSpec as P

epsilon = 1e-06
WIDE = 512
f32 = jnp.float32
bf16 = jnp.bfloat16
MESH = pl.DeviceIdType.MESH


def halves(x):
    high = x.astype(bf16)
    return high, (x - high.astype(f32)).astype(bf16)


def left_parts(x):
    high, low = halves(x)
    return jnp.concatenate([high, low, high], axis=0)


def right_parts(x):
    high, low = halves(x)
    return jnp.concatenate([high, high, low], axis=0)


def dot_nn(a, b):
    return lax.dot_general(a, b, (((1,), (0,)), ((), ())), preferred_element_type=f32)


def dot_nt(a, b):
    return lax.dot_general(a, b, (((1,), (1,)), ((), ())), preferred_element_type=f32)


def dot_tn(a, b):
    return lax.dot_general(a, b, (((0,), (0,)), ((), ())), preferred_element_type=f32)


def over_pixels(a, b):
    a_high, a_low = halves(a)
    b_high, b_low = halves(b)
    return dot_nt(
        jnp.concatenate([a_high, a_low, a_high], axis=1),
        jnp.concatenate([b_high, b_high, b_low], axis=1),
    )


def fold(x):
    return x[:, :128] + x[:, 128:256] + x[:, 256:384] + x[:, 384:]


class Link:
    def __init__(self, copy, sends=None, receives=None):
        self.copy, self.sends, self.receives = copy, sends, receives
        if sends is None:
            copy.start()
        else:
            pl.when(sends)(copy.start)

    def wait(self):
        if self.sends is None:
            self.copy.wait()
        else:
            pl.when(self.receives)(self.copy.wait_recv)
            pl.when(self.sends)(self.copy.wait_send)


def normed(x):
    center = x - jnp.mean(x, axis=0, keepdims=True)
    scale = 1.0 / jnp.sqrt(jnp.mean(center * center, axis=0, keepdims=True) + epsilon)
    return center * scale, scale


def normed_back(grad, value, scale):
    return scale * (
        grad
        - jnp.mean(grad, axis=0, keepdims=True)
        - value * jnp.mean(grad * value, axis=0, keepdims=True)
    )


def block_kernel(sizes, factor, area, cols, *refs):
    operands, results, refs = refs[:14], refs[14:18], refs[18:]
    out_ref, grad_ref, early_ref, late_ref = results
    (
        x_in, c_in, expand_w, taps_w, pool_w, bias_w, squeeze_w, branch_w,
        up_w, down_w, scale_w, query_w, value_w, cross_w,
    ) = refs[:14]
    (
        x_s, c_s, cp_s, n0_s, s0_s, d_s, cv_s, g_s, t_s, n1_s, s1_s, e_s, u_s, h_s,
        hp_s, dh_s, dhp_s, o_s, op_s, dg_s, dr_s, de_s, dcv_s, e_att, att_s, attn_s, atts_s,
        taps_s, fold_s, tap_acc, queryp_s, valuep_s, crossp_s, pool_s, poolg_s,
        early, late, early_1, early_2, early_3, late_1, late_2, late_3,
        expand_f, expand_b, squeeze_f, squeeze_b, up_f, up_b, down_f, down_b,
        query_f, query_b, value_f, value_b,
        loads, sends, recvs, group_sends, group_recvs,
    ) = refs[14:]
    rows, lanes = sizes
    row = lax.axis_index("row")
    view = lax.axis_index("view")
    lane = lax.axis_index("dp") * 2 + view
    mine = (3 * view, 1 + view)
    theirs = (3 - 3 * view, 2 - view)
    slots = (view, 1 - view)
    edge = view * (rows - 1)
    other_edge = rows - 1 - edge

    def in_row(step):
        return {"row": lax.rem(row + step, rows)}

    def in_lane(step):
        other = lax.rem(lane + step, lanes)
        return {"dp": other // 2, "view": lax.rem(other, 2)}

    above = in_row(rows - 1)
    below = in_row(1)
    mine_side = in_row((1 - view) * (rows - 1) + view)
    theirs_side = in_row(view * (rows - 1) + 1 - view)
    partner = {"view": 1 - view}

    barrier = pltpu.get_barrier_semaphore()
    for step in range(1, rows):
        pl.semaphore_signal(barrier, inc=1, device_id=in_row(step), device_id_type=MESH)
    for step in range(1, lanes):
        pl.semaphore_signal(barrier, inc=1, device_id=in_lane(step), device_id_type=MESH)

    local = [
        pltpu.make_async_copy(operands[item], refs[item], loads.at[item]) for item in range(14)
    ]
    for item in (0, 2, 3, 4, 5, 6, 7, 8, 9, 10, 11, 12, 13, 1):
        local[item].start()

    def send(index, source, target, device, *when):
        return Link(
            pltpu.make_async_remote_copy(
                src_ref=source,
                dst_ref=target,
                send_sem=sends.at[index],
                recv_sem=recvs.at[index],
                device_id=device,
                device_id_type=MESH,
            ),
            *when,
        )

    def spread(phase, source, target, device, count):
        return [
            Link(
                pltpu.make_async_remote_copy(
                    src_ref=source(step),
                    dst_ref=target,
                    send_sem=group_sends.at[phase, step - 1],
                    recv_sem=group_recvs.at[phase, step - 1],
                    device_id=device(step),
                    device_id_type=MESH,
                )
            )
            for step in range(1, count)
        ]

    def finish(links):
        for link in links:
            link.wait()

    for h in range(4):
        x_s[h + 1, :, 384:] = jnp.zeros((64, 128), f32)
    local[0].wait()
    for h in (0, 3, 1, 2):
        x_s[h + 1, :, :cols] = x_in[:, h, :]

    pl.semaphore_wait(barrier, rows + lanes - 2)
    halo_up = send(0, x_s.at[1], x_s.at[5], above, row != 0, row != rows - 1)
    halo_down = send(1, x_s.at[4], x_s.at[0], below, row != rows - 1, row != 0)

    def forward_parts(transposed):
        return left_parts(transposed).astype(f32).T.astype(bf16)

    for item in range(2, 14):
        local[item].wait()
    weights_sent = [
        send(2, query_w, queryp_s, partner),
        send(3, value_w, valuep_s, partner),
        send(4, cross_w, crossp_s, partner),
    ]
    expand_f[...] = forward_parts(expand_w[...])

    def expand_row(h):
        value, scale = normed(x_s[h])
        d_s[h] = dot_nn(expand_f[...], right_parts(value))
        return value, scale

    @pl.loop(1, 5)
    def _(h):
        value, scale = expand_row(h)
        n0_s[h - 1] = value
        s0_s[h - 1] = scale

    tap_rows = jnp.concatenate(
        [taps_w[i, j : j + 1, :] for i in range(3) for j in range(3)]
        + [jnp.zeros((7, 128), f32)],
        axis=0,
    )
    tap_columns = tap_rows.T
    for tap in range(9):
        taps_s[tap] = jnp.broadcast_to(tap_columns[:, tap : tap + 1], (128, 128))
    for h in range(4):
        c_s[h, :, 384:] = jnp.zeros((64, 128), f32)
    local[1].wait()
    for h in range(4):
        c_s[h, :, :cols] = c_in[:, h, :]

    halo_up.wait()
    halo_down.wait()

    @pl.when(row == 0)
    def _():
        x_s[0] = jnp.zeros((64, WIDE), f32)

    @pl.when(row == rows - 1)
    def _():
        x_s[5] = jnp.zeros((64, WIDE), f32)

    cotangent_sent = send(5, c_s.at[pl.ds(2 - 2 * view, 2)], cp_s, partner)
    expand_row(0)
    expand_row(5)

    inside = lax.broadcasted_iota(jnp.int32, (1, WIDE), 1) < cols
    fold_s[...] = jnp.zeros_like(fold_s)

    def tap_at(tap, start, size):
        piece = taps_s[tap, pl.ds(start, size), :]
        return jnp.concatenate([piece] * 4, axis=1)

    @pl.loop(1, 5)
    def _(h):
        for start in range(0, 128, 16):
            columns = [jnp.zeros((16, WIDE), f32)] * 3
            for i in range(3):
                value = d_s[h + i - 1, start : start + 16, :]
                for j in range(3):
                    columns[j] = columns[j] + tap_at(3 * i + j, start, 16) * value
            total = columns[1] + pltpu.roll(columns[0], 1, 1) + pltpu.roll(columns[2], WIDE - 1, 1)
            cv_s[h, start : start + 16, :] = jnp.where(inside, total, 0.0)
        gate = cv_s[h, :64, :] * cv_s[h, 64:, :]
        g_s[h - 1] = gate
        fold_s[0] += fold(gate)

    eye = lax.broadcasted_iota(jnp.int32, (64, 128), 0) == lax.broadcasted_iota(
        jnp.int32, (64, 128), 1
    )

    def to_column(vector):
        spread_out = jnp.broadcast_to(vector, (64, vector.shape[1]))
        return jnp.sum(
            jnp.where(eye[:, : vector.shape[1]], spread_out, 0.0), axis=1, keepdims=True
        )

    def to_row(column):
        return jnp.sum(
            jnp.where(eye, jnp.broadcast_to(column, (64, 128)), 0.0), axis=0, keepdims=True
        )

    pool_s[row] = to_row(jnp.sum(fold_s[0], axis=1, keepdims=True))
    links = spread(0, lambda step: pool_s.at[row], pool_s.at[row], in_row, rows)
    expand_b[...] = forward_parts(expand_w[...].T)
    up_f[...] = forward_parts(up_w[...])
    up_b[...] = forward_parts(up_w[...].T)
    for weight, forward, backward in (
        (squeeze_w, squeeze_f, squeeze_b),
        (down_w, down_f, down_b),
        (query_w, query_f.at[0], query_b.at[0]),
        (value_w, value_f.at[0], value_b.at[0]),
    ):
        forward[...] = forward_parts(weight[...].T)
        backward[...] = forward_parts(weight[...])
    bias = to_column(bias_w[...])
    branch = to_column(branch_w[...])
    ffn_scale = to_column(scale_w[...])
    cross = to_column(cross_w[...])
    tap_acc[...] = jnp.zeros_like(tap_acc)
    finish(links)

    conv_up = send(6, cv_s.at[1], cv_s.at[5], above, row != 0, row != rows - 1)
    conv_down = send(7, cv_s.at[4], cv_s.at[0], below, row != rows - 1, row != 0)
    pooled = jnp.sum(pool_s[...], axis=0) / area
    attention = jnp.sum(pool_w[...] * pooled[:, :64], axis=1, keepdims=True) + bias

    def tail_row(h):
        squeezed = dot_nn(squeeze_f[...], right_parts(g_s[h] * attention))
        t_s[h] = squeezed
        residual = x_s[h + 1] + branch * squeezed
        value, scale = normed(residual)
        n1_s[h] = value
        s1_s[h] = scale
        expanded = dot_nn(up_f[...], right_parts(value))
        e_s[h] = expanded
        shrunk = dot_nn(down_f[...], right_parts(expanded[:64] * expanded[64:]))
        u_s[h] = shrunk
        h_s[h] = residual + ffn_scale * shrunk

    hidden_sent = []
    for k in range(2):
        tail_row(theirs[k])
        hidden_sent.append(send(8 + k, h_s.at[theirs[k]], hp_s.at[k], partner))
    for k in range(2):
        tail_row(mine[k])

    finish(weights_sent)
    query_f[1] = forward_parts(queryp_s[...].T)
    query_b[1] = forward_parts(queryp_s[...])
    value_f[1] = forward_parts(valuep_s[...].T)
    value_b[1] = forward_parts(valuep_s[...])
    crossp = to_column(crossp_s[...])
    cotangent_sent.wait()

    sixteen = lax.broadcasted_iota(jnp.int32, (16, WIDE), 0)
    outside16 = lax.broadcasted_iota(jnp.int32, (16, WIDE), 1) >= cols
    ones16 = jnp.ones((16, WIDE), bf16)
    mask_left = jnp.where(
        sixteen == 0, jnp.where(outside16, -256.0, 0.0), jnp.where(sixteen == 1, 1.0, 0.0)
    ).astype(bf16)
    mask_right = jnp.where(
        sixteen == 0, 1.0, jnp.where((sixteen == 1) & outside16, -256.0, 0.0)
    ).astype(bf16)

    def attend_row(k):
        own, other = h_s[mine[k]], hp_s[k]
        own_up, other_up = c_s[mine[k]], cp_s[slots[k]]
        own_n, own_scale = normed(own)
        other_n, other_scale = normed(other)
        attn_s[k, 0] = own_n
        attn_s[k, 1] = other_n
        atts_s[k] = own_scale
        own_q = dot_nn(query_f[0], right_parts(own_n))
        other_q = dot_nn(query_f[1], right_parts(other_n))
        own_v = dot_nn(value_f[0], right_parts(own))
        other_v = dot_nn(value_f[1], right_parts(other))
        scores = dot_tn(
            jnp.concatenate([left_parts(own_q * 0.125), mask_left], axis=0),
            jnp.concatenate([right_parts(other_q), mask_right], axis=0),
        )
        weights = jnp.exp(scores)
        e_att[...] = weights
        w_high, w_low = halves(weights)

        def weighted(dot, values):
            high, low = halves(values)
            large = dot(jnp.concatenate([high, ones16, low], axis=0), w_high)
            small = dot(jnp.concatenate([high, ones16], axis=0), w_low)
            bottom = jnp.where(inside, large[64:65] + small[64:65], 1.0)
            return large[:64] + large[80:] + small[:64], 1.0 / bottom

        def through(dot, values, high_m, low_m):
            high, low = halves(values)
            large = dot(jnp.concatenate([high, low], axis=0), high_m)
            return large[:64] + large[64:] + dot(high, low_m)

        own_c, own_r = weighted(dot_nt, other_v)
        other_c, other_r = weighted(dot_nn, own_v)
        own_c = own_c * own_r
        other_c = other_c * other_r
        o_s[mine[k]] = own + cross * own_c
        op_s[k] = other + crossp * other_c
        own_d = cross * own_up * own_r
        other_d = crossp * other_up * other_r
        fold_s[4] += fold(own_up * own_c)
        fold_s[5] += fold(other_up * other_c)
        own_delta, own_delta_low = halves(-jnp.sum(own_d * own_c, axis=0, keepdims=True))
        other_delta, other_delta_low = halves(-jnp.sum(other_d * other_c, axis=0, keepdims=True))
        left_tail = jnp.where(
            sixteen == 0,
            own_delta.astype(f32),
            jnp.where(
                sixteen == 1, own_delta_low.astype(f32), jnp.where(sixteen < 4, 1.0, 0.0)
            ),
        ).astype(bf16)
        right_tail = jnp.where(
            sixteen == 2,
            other_delta.astype(f32),
            jnp.where(
                sixteen == 3, other_delta_low.astype(f32), jnp.where(sixteen < 2, 1.0, 0.0)
            ),
        ).astype(bf16)
        change = dot_tn(
            jnp.concatenate(
                [left_parts(jnp.concatenate([own_d, own_v], axis=0)), left_tail], axis=0
            ),
            jnp.concatenate(
                [right_parts(jnp.concatenate([other_v, other_d], axis=0)), right_tail], axis=0
            ),
        )
        ds_high, ds_low = halves(e_att[...] * change * 0.125)
        other_dv = through(dot_nn, own_d, w_high, w_low)
        other_dq = through(dot_nn, own_q, ds_high, ds_low)
        dn = dot_nn(query_b[1], right_parts(other_dq))
        dhp_s[k] = (
            other_up
            + dot_nn(value_b[1], right_parts(other_dv))
            + normed_back(dn, other_n, other_scale)
        )
        att_s[k, 1] = other_dq
        att_s[k, 3] = other_dv
        att_s[k, 2] = through(dot_nt, other_d, w_high, w_low)
        att_s[k, 0] = through(dot_nt, other_q, ds_high, ds_low)

    def own_back(k):
        dn = dot_nn(query_b[0], right_parts(att_s[k, 0]))
        dh_s[mine[k]] = (
            c_s[mine[k]]
            + dot_nn(value_b[0], right_parts(att_s[k, 2]))
            + normed_back(dn, attn_s[k, 0], atts_s[k])
        )

    returned = []
    for k in range(2):
        hidden_sent[k].wait()
        attend_row(k)
        returned.append(send(10 + k, dhp_s.at[k], dh_s.at[mine[k]], partner))

    def tail_back_row(h):
        up = dh_s[h]
        expanded = e_s[h]
        dgate = dot_nn(down_b[...], right_parts(ffn_scale * up))
        de = jnp.concatenate([dgate * expanded[64:], dgate * expanded[:64]], axis=0)
        de_s[h] = de
        dn = dot_nn(up_b[...], right_parts(de))
        dr = up + normed_back(dn, n1_s[h], s1_s[h])
        dr_s[h] = dr
        dscaled = dot_nn(squeeze_b[...], right_parts(branch * dr))
        fold_s[3] += fold(dscaled * g_s[h])
        dg_s[h + 1] = dscaled * attention

    own_back(0)
    tail_back_row(mine[0])
    gate_mine = send(
        12, dg_s.at[mine[0] + 1], dg_s.at[5 - 5 * view], mine_side, row != edge, row != other_edge
    )
    own_back(1)
    tail_back_row(mine[1])

    returned[0].wait()
    tail_back_row(theirs[0])
    gate_theirs = send(
        13, dg_s.at[theirs[0] + 1], dg_s.at[5 * view], theirs_side, row != other_edge, row != edge
    )
    returned[1].wait()
    tail_back_row(theirs[1])

    d_attention = jnp.sum(fold_s[3], axis=1, keepdims=True)
    poolg_s[row, :, :64] = jnp.sum(pool_w[...] * d_attention, axis=0, keepdims=True)
    poolg_s[row, :, 64:] = jnp.zeros((1, 64), f32)
    links = spread(1, lambda step: poolg_s.at[row], poolg_s.at[row], in_row, rows)
    out_sent = [send(14 + k, op_s.at[k], o_s.at[mine[k]], partner) for k in range(2)]

    query_grads = [jnp.zeros((64, 64), f32)] * 4
    for k in range(2):
        fields = (attn_s[k, 0], attn_s[k, 1], h_s[mine[k]], hp_s[k])
        for item in range(4):
            query_grads[item] = query_grads[item] + over_pixels(att_s[k, item], fields[item])
    for start, pair in ((128, query_grads[:2]), (192, query_grads[2:])):
        early[start : start + 64, :64] = jnp.where(view == 0, pair[0], pair[1])
        early[start : start + 64, 64:] = jnp.where(view == 0, pair[1], pair[0])
    early[:128, :] = jnp.zeros((128, 128), f32)

    @pl.loop(0, 4)
    def _(h):
        up = dh_s[h]
        dr = dr_s[h]
        fold_s[1] += fold(up * u_s[h])
        fold_s[2] += fold(dr * t_s[h])
        expanded = e_s[h]
        early[:64, :] += over_pixels(n1_s[h], de_s[h])
        early[64:128, :64] += over_pixels(branch * dr, g_s[h] * attention)
        early[64:128, 64:] += over_pixels(ffn_scale * up, expanded[:64] * expanded[64:])

    finish(links)

    early_size, late_size = 256 // rows, 128 // rows

    def chunk_at(index, size):
        return pl.ds(pl.multiple_of(index * size, 8), size)

    links = spread(
        2,
        lambda step: early.at[chunk_at(lax.rem(row + step, rows), early_size)],
        early_1.at[row],
        in_row,
        rows,
    )
    early_1[row] = early[chunk_at(row, early_size), :]
    constant = to_column(jnp.sum(poolg_s[...], axis=0) / area)

    def gate_back_row(h):
        total = dg_s[h] + constant
        dcv_s[h, :64, :] = total * cv_s[h, 64:, :]
        dcv_s[h, 64:, :] = total * cv_s[h, :64, :]

    pl.loop(1, 5)(gate_back_row)
    gate_mine.wait()
    gate_theirs.wait()
    conv_up.wait()
    conv_down.wait()
    for outer, limit in ((0, 0), (5, rows - 1)):

        @pl.when(row == limit)
        def _():
            dcv_s[outer] = jnp.zeros((128, WIDE), f32)

        @pl.when(row != limit)
        def _():
            gate_back_row(outer)

    @pl.loop(0, 8)
    def _(chunk):
        start = pl.multiple_of(chunk * 16, 16)
        size = 16
        for h in range(1, 5):
            center = dcv_s[h, pl.ds(start, size), :]
            moved = [pltpu.roll(center, WIDE - 1, 1), center, pltpu.roll(center, 1, 1)]
            for i in range(3):
                value = d_s[h + i - 1, pl.ds(start, size), :]
                for j in range(3):
                    tap_acc[3 * i + j, pl.ds(start, size), :] += fold(moved[j] * value)
        for h in range(1, 5):
            columns = [jnp.zeros((size, WIDE), f32)] * 3
            for i in range(3):
                value = dcv_s[h - i + 1, pl.ds(start, size), :]
                for j in range(3):
                    columns[j] = columns[j] + tap_at(3 * i + j, start, size) * value
            cv_s[h, pl.ds(start, size), :] = (
                columns[1] + pltpu.roll(columns[2], 1, 1) + pltpu.roll(columns[0], WIDE - 1, 1)
            )

    finish(links)

    early_2[lane] = jnp.sum(early_1[...], axis=0)
    early_links = spread(3, lambda step: early_2.at[lane], early_2.at[lane], in_lane, lanes)

    late[:64, :] = jnp.zeros((64, 128), f32)

    @pl.loop(0, 4)
    def _(h):
        late[:64, :] += over_pixels(n0_s[h], cv_s[h + 1])

    place = lax.broadcasted_iota(jnp.int32, (64, 128), 1)

    def columns_of(value):
        return jnp.sum(value, axis=1, keepdims=True)

    items = [columns_of(tap_acc[tap, :64, :]) for tap in range(9)]
    items += [columns_of(tap_acc[tap, 64:, :]) for tap in range(9)]
    items += [d_attention, columns_of(fold_s[2]), columns_of(fold_s[1])]
    own_cross = columns_of(fold_s[4])
    other_cross = columns_of(fold_s[5])
    items.append(jnp.where(view == 0, own_cross, other_cross))
    items.append(jnp.where(view == 0, other_cross, own_cross))
    mixed = d_attention * pooled
    for index, item in enumerate(items):
        mixed = jnp.where(place == 64 + index, item, mixed)
    late[64:, :] = mixed

    late_links = spread(
        5,
        lambda step: late.at[chunk_at(lax.rem(row + step, rows), late_size)],
        late_1.at[row],
        in_row,
        rows,
    )
    late_1[row] = late[chunk_at(row, late_size), :]

    @pl.loop(0, 4)
    def _(h):
        dn = dot_nn(expand_b[...], right_parts(cv_s[h + 1]))
        dr_s[h] = dr_s[h] + normed_back(dn, n0_s[h], s0_s[h])

    finish(early_links)
    early_3[row] = jnp.sum(early_2[...], axis=0) * factor
    early_links = spread(4, lambda step: early_3.at[row], early_3.at[row], in_row, rows)
    finish(late_links)

    late_2[lane] = jnp.sum(late_1[...], axis=0)
    late_links = spread(6, lambda step: late_2.at[lane], late_2.at[lane], in_lane, lanes)
    for h in range(4):
        grad_ref[:, h, :] = dr_s[h, :, :cols]
    finish(out_sent)
    finish(late_links)

    late_3[row] = jnp.sum(late_2[...], axis=0) * factor
    late_links = spread(7, lambda step: late_3.at[row], late_3.at[row], in_row, rows)
    for h in range(4):
        out_ref[:, h, :] = o_s[h, :, :cols]
    finish(early_links)
    early_ref[...] = early_3[...]
    finish(late_links)
    late_ref[...] = late_3[...]


def format_kernel(out_in, grad_in, early_ref, late_ref, *refs):
    (
        out_ref, grad_ref, expand_ref, taps_ref, pool_ref, bias_ref, squeeze_ref, branch_ref,
        up_ref, down_ref, scale_ref, query_ref, value_ref, cross_ref, sems,
    ) = refs
    copies = [
        pltpu.make_async_copy(out_in, out_ref, sems.at[0]),
        pltpu.make_async_copy(grad_in, grad_ref, sems.at[1]),
    ]
    for copy in copies:
        copy.start()
    view = lax.axis_index("view")
    up_ref[...] = early_ref[:64, :]
    middle = early_ref[64:128, :]
    squeeze_ref[...] = middle[:, :64]
    down_ref[...] = middle[:, 64:]
    for start, target in ((128, query_ref), (192, value_ref)):
        both = early_ref[start : start + 64, :]
        target[...] = jnp.where(view == 0, both[:, :64], both[:, 64:])
    expand_ref[...] = late_ref[:64, :]
    mixed = late_ref[64:, :]
    pool_ref[...] = mixed[:, :64]
    turned = mixed.T
    for tap in range(9):
        taps_ref[tap // 3, tap % 3 : tap % 3 + 1, :64] = turned[64 + tap : 65 + tap, :]
        taps_ref[tap // 3, tap % 3 : tap % 3 + 1, 64:] = turned[73 + tap : 74 + tap, :]
    for place, target in ((82, bias_ref), (83, branch_ref), (84, scale_ref)):
        target[...] = turned[place : place + 1, :]
    cross_ref[...] = jnp.where(view == 0, turned[85:86, :], turned[86:87, :])
    for copy in copies:
        copy.wait()


def per_device(rows, lanes, *arrays):
    cols = arrays[0].shape[4]
    area = 4 * rows * cols
    factor = (lanes * area) ** (-0.5)
    wide = functools.partial(jax.ShapeDtypeStruct, dtype=f32)

    def fields(*shape):
        return pltpu.VMEM(shape, f32)

    def parts(*shape):
        return pltpu.VMEM(shape, bf16)

    operands = [
        arrays[0][0, 0],
        arrays[1][0, 0],
        arrays[2].T,
        arrays[3].transpose(1, 2, 0),
        arrays[4],
        arrays[5][None],
        arrays[6],
        arrays[7][None],
        arrays[8].T,
        arrays[9],
        arrays[10][None],
        arrays[11][0],
        arrays[12][0],
        arrays[13],
    ]
    early_size, late_size = 256 // rows, 128 // rows
    scratch = [fields(*operand.shape) for operand in operands] + [
        fields(6, 64, WIDE),
        fields(4, 64, WIDE),
        fields(2, 64, WIDE),
        fields(4, 64, WIDE),
        fields(4, 1, WIDE),
        fields(6, 128, WIDE),
        fields(6, 128, WIDE),
        fields(4, 64, WIDE),
        fields(4, 64, WIDE),
        fields(4, 64, WIDE),
        fields(4, 1, WIDE),
        fields(4, 128, WIDE),
        fields(4, 64, WIDE),
        fields(4, 64, WIDE),
        fields(2, 64, WIDE),
        fields(4, 64, WIDE),
        fields(2, 64, WIDE),
        fields(4, 64, WIDE),
        fields(2, 64, WIDE),
        fields(6, 64, WIDE),
        fields(4, 64, WIDE),
        fields(4, 128, WIDE),
        fields(6, 128, WIDE),
        fields(WIDE, WIDE),
        fields(2, 4, 64, WIDE),
        fields(2, 2, 64, WIDE),
        fields(2, 1, WIDE),
        fields(9, 128, 128),
        fields(6, 64, 128),
        fields(9, 128, 128),
        fields(64, 64),
        fields(64, 64),
        fields(1, 64),
        fields(rows, 1, 128),
        fields(rows, 1, 128),
        fields(256, 128),
        fields(128, 128),
        fields(rows, early_size, 128),
        fields(lanes, early_size, 128),
        fields(rows, early_size, 128),
        fields(rows, late_size, 128),
        fields(lanes, late_size, 128),
        fields(rows, late_size, 128),
        parts(128, 192),
        parts(64, 384),
        parts(64, 192),
        parts(64, 192),
        parts(128, 192),
        parts(64, 384),
        parts(64, 192),
        parts(64, 192),
        parts(2, 64, 192),
        parts(2, 64, 192),
        parts(2, 64, 192),
        parts(2, 64, 192),
        pltpu.SemaphoreType.DMA((14,)),
        pltpu.SemaphoreType.DMA((16,)),
        pltpu.SemaphoreType.DMA((16,)),
        pltpu.SemaphoreType.DMA((8, 15)),
        pltpu.SemaphoreType.DMA((8, 15)),
    ]
    in_place = pl.BlockSpec(memory_space=pl.ANY)
    in_vmem = pl.BlockSpec(memory_space=pltpu.VMEM)
    out, grad, early, late = pl.pallas_call(
        functools.partial(block_kernel, (rows, lanes), factor, area, cols),
        out_shape=(
            wide((64, 4, cols)),
            wide((64, 4, cols)),
            wide((rows, early_size, 128)),
            wide((rows, late_size, 128)),
        ),
        in_specs=[in_place] * 14,
        out_specs=(in_vmem,) * 4,
        scratch_shapes=scratch,
        compiler_params=pltpu.CompilerParams(
            collective_id=0, has_side_effects=True, vmem_limit_bytes=56 * 2**20
        ),
    )(*operands)
    shapes = [operand.shape for operand in operands]
    done = pl.pallas_call(
        format_kernel,
        out_shape=[wide(shape) for shape in shapes],
        in_specs=[in_place, in_place, in_vmem, in_vmem],
        out_specs=[in_place, in_place] + [in_vmem] * 12,
        scratch_shapes=[pltpu.SemaphoreType.DMA((2,))],
    )(out, grad, early.reshape(256, 128), late.reshape(128, 128))
    return (
        done[0][None, None],
        done[1][None, None],
        done[2].T,
        done[3].transpose(2, 0, 1),
        done[4],
        done[5][0],
        done[6],
        done[7][0],
        done[8].T,
        done[9],
        done[10][0],
        done[11][None],
        done[12][None],
        done[13],
    )


def solution(mesh):
    field = P("view", "dp", None, "row", None)
    copied = (P(),) * 9
    owned = (P("view", None, None), P("view", None, None), P("view", None))
    return jax.shard_map(
        functools.partial(per_device, mesh.shape["row"], 2 * mesh.shape["dp"]),
        mesh=mesh,
        in_specs=(field, field) + copied + owned,
        out_specs=(field, field) + copied + owned,
        check_vma=False,
    )
```

time: 95.3 us -> 114 us (1.20)
  Pallas kernels: 82 us -> 113 us
  local copies, waits for them, and re-layouts: 11.9 us -> 0 us
    pallas_call x0 -> x1, Pallas kernels: none -> 34.5 us  [per_device(): pl.pallas_call(format_kernel, out_shape=[wide(shape) for shape in shapes]...]
    unnamed x14 -> x0, local copies, waits for them, and re-layouts: 6.05 us -> none
    pallas_call x1, Pallas kernels: 82 us -> 78.8 us  [per_device(): pl.pallas_call(functools.partial(block_kernel, (rows, lanes), factor, are...]
    slice x7 -> x0, local copies, waits for them, and re-layouts: 2.35 us -> none  [the longest x1 0.73 us: per_device(): mixed[:, 84]]
    reshape x4 -> x0, local copies, waits for them, and re-layouts: 1.5 us -> none  [the longest x2 0.75 us: per_device(): conv_kernel.reshape(128, 9)]
    broadcast_in_dim x1 -> x0, local copies, waits for them, and re-layouts: 1.27 us -> none  [placed(): return value[:, :, :cols].transpose(1, 0, 2)[None, None]]
where the time goes in v1:
time: 114 us
  Pallas kernels  113 us (99%)
    pallas_call x1, Pallas kernels, per_device(): pl.pallas_call(functools.partial(block_kernel, (rows, lanes), factor, are...  78.8 us
    pallas_call x1, Pallas kernels, per_device(): pl.pallas_call(format_kernel, out_shape=[wide(shape) for shape in shapes]...  34.5 us

profile of v1, /device:TPU:1, one launch (start us, length us, event | category | flops | bytes accessed | tf_op | source)
XLA Modules:
  0.0 113.9 jit_solution(7560835989307586269)
XLA Ops:
  0.7 78.8 %shard_map.245 = (f32[64,4,480]{2,1,0:T(4,128)}, f32[64,4,480]{2,1,0:T(4,128)}, f32[16,16,128]{2,1,0:T(8,128)}, f32[16,8,128]{2,1,0:T(8,128)}) custom-call(f32[64,4,480]{2,1,0:T(4,128)} %bitcast.22, f32[64,4,480]{2,1,0:T(4,128)} %bitcast.23, f32[64,128]{1,0:T(8,128)} %bitcast.26, f32[3,3,128]{2,1,0:T(4,128)} %bitcast.30, f32[64,64]{1,0:T(8,128)} %refs_4_.1, ...), custom_call_target="tpu_custom_call" | custom-call | tf_op jit(solution)/shard_map/pallas_call | solution.py:729
  79.4 34.5 %shard_map.246 = (f32[64,4,480]{2,1,0:T(4,128)}, f32[64,4,480]{2,1,0:T(4,128)}, f32[64,128]{1,0:T(8,128)}, f32[3,3,128]{2,1,0:T(4,128)}, f32[64,64]{1,0:T(8,128)...) custom-call(f32[64,4,480]{2,1,0:T(4,128)} %get-tuple-element.32.out_, ...), custom_call_target="tpu_custom_call" | custom-call | tf_op jit(solution)/shard_map/pallas_call | solution.py:745

commit v2 on v1

--- a/solution.py
+++ b/solution.py
@@ -366,6 +366,8 @@
         other_c = other_c * other_r
         o_s[mine[k]] = own + cross * own_c
         op_s[k] = other + crossp * other_c
+        if k == 0:
+            out_sent.append(send(14, op_s.at[0], o_s.at[mine[0]], partner))
         own_d = cross * own_up * own_r
         other_d = crossp * other_up * other_r
         fold_s[4] += fold(own_up * own_c)
@@ -417,6 +419,7 @@
         )
 
     returned = []
+    out_sent = []
     for k in range(2):
         hidden_sent[k].wait()
         attend_row(k)
@@ -455,7 +458,7 @@
     poolg_s[row, :, :64] = jnp.sum(pool_w[...] * d_attention, axis=0, keepdims=True)
     poolg_s[row, :, 64:] = jnp.zeros((1, 64), f32)
     links = spread(1, lambda step: poolg_s.at[row], poolg_s.at[row], in_row, rows)
-    out_sent = [send(14 + k, op_s.at[k], o_s.at[mine[k]], partner) for k in range(2)]
+    out_sent.append(send(15, op_s.at[1], o_s.at[mine[1]], partner))
 
     query_grads = [jnp.zeros((64, 64), f32)] * 4
     for k in range(2):
@@ -478,14 +481,12 @@
         early[64:128, :64] += over_pixels(branch * dr, g_s[h] * attention)
         early[64:128, 64:] += over_pixels(ffn_scale * up, expanded[:64] * expanded[64:])
 
-    finish(links)
-
-    early_size, late_size = 256 // rows, 128 // rows
+    early_size, late_size = 256 // rows, 128 // lanes
 
     def chunk_at(index, size):
         return pl.ds(pl.multiple_of(index * size, 8), size)
 
-    links = spread(
+    early_links = spread(
         2,
         lambda step: early.at[chunk_at(lax.rem(row + step, rows), early_size)],
         early_1.at[row],
@@ -493,6 +494,8 @@
         rows,
     )
     early_1[row] = early[chunk_at(row, early_size), :]
+    finish(links)
+
     constant = to_column(jnp.sum(poolg_s[...], axis=0) / area)
 
     def gate_back_row(h):
@@ -536,7 +539,7 @@
                 columns[1] + pltpu.roll(columns[2], 1, 1) + pltpu.roll(columns[0], WIDE - 1, 1)
             )
 
-    finish(links)
+    finish(early_links)
 
     early_2[lane] = jnp.sum(early_1[...], axis=0)
     early_links = spread(3, lambda step: early_2.at[lane], early_2.at[lane], in_lane, lanes)
@@ -566,12 +569,12 @@
 
     late_links = spread(
         5,
-        lambda step: late.at[chunk_at(lax.rem(row + step, rows), late_size)],
-        late_1.at[row],
-        in_row,
-        rows,
-    )
-    late_1[row] = late[chunk_at(row, late_size), :]
+        lambda step: late.at[chunk_at(lax.rem(lane + step, lanes), late_size)],
+        late_1.at[lane],
+        in_lane,
+        lanes,
+    )
+    late_1[lane] = late[chunk_at(lane, late_size), :]
 
     @pl.loop(0, 4)
     def _(h):
@@ -583,15 +586,15 @@
     early_links = spread(4, lambda step: early_3.at[row], early_3.at[row], in_row, rows)
     finish(late_links)
 
-    late_2[lane] = jnp.sum(late_1[...], axis=0)
-    late_links = spread(6, lambda step: late_2.at[lane], late_2.at[lane], in_lane, lanes)
+    late_2[row] = jnp.sum(late_1[...], axis=0)
+    late_links = spread(6, lambda step: late_2.at[row], late_2.at[row], in_row, rows)
     for h in range(4):
         grad_ref[:, h, :] = dr_s[h, :, :cols]
     finish(out_sent)
     finish(late_links)
 
-    late_3[row] = jnp.sum(late_2[...], axis=0) * factor
-    late_links = spread(7, lambda step: late_3.at[row], late_3.at[row], in_row, rows)
+    late_3[lane] = jnp.sum(late_2[...], axis=0) * factor
+    late_links = spread(7, lambda step: late_3.at[lane], late_3.at[lane], in_lane, lanes)
     for h in range(4):
         out_ref[:, h, :] = o_s[h, :, :cols]
     finish(early_links)
@@ -603,14 +606,10 @@
 def format_kernel(out_in, grad_in, early_ref, late_ref, *refs):
     (
         out_ref, grad_ref, expand_ref, taps_ref, pool_ref, bias_ref, squeeze_ref, branch_ref,
-        up_ref, down_ref, scale_ref, query_ref, value_ref, cross_ref, sems,
+        up_ref, down_ref, scale_ref, query_ref, value_ref, cross_ref,
     ) = refs
-    copies = [
-        pltpu.make_async_copy(out_in, out_ref, sems.at[0]),
-        pltpu.make_async_copy(grad_in, grad_ref, sems.at[1]),
-    ]
-    for copy in copies:
-        copy.start()
+    out_ref[...] = out_in[...]
+    grad_ref[...] = grad_in[...]
     view = lax.axis_index("view")
     up_ref[...] = early_ref[:64, :]
     middle = early_ref[64:128, :]
@@ -629,8 +628,6 @@
     for place, target in ((82, bias_ref), (83, branch_ref), (84, scale_ref)):
         target[...] = turned[place : place + 1, :]
     cross_ref[...] = jnp.where(view == 0, turned[85:86, :], turned[86:87, :])
-    for copy in copies:
-        copy.wait()
 
 
 def per_device(rows, lanes, *arrays):
@@ -661,7 +658,7 @@
         arrays[12][0],
         arrays[13],
     ]
-    early_size, late_size = 256 // rows, 128 // rows
+    early_size, late_size = 256 // rows, 128 // lanes
     scratch = [fields(*operand.shape) for operand in operands] + [
         fields(6, 64, WIDE),
         fields(4, 64, WIDE),
@@ -703,9 +700,9 @@
         fields(rows, early_size, 128),
         fields(lanes, early_size, 128),
         fields(rows, early_size, 128),
+        fields(lanes, late_size, 128),
         fields(rows, late_size, 128),
         fields(lanes, late_size, 128),
-        fields(rows, late_size, 128),
         parts(128, 192),
         parts(64, 384),
         parts(64, 192),
@@ -732,7 +729,7 @@
             wide((64, 4, cols)),
             wide((64, 4, cols)),
             wide((rows, early_size, 128)),
-            wide((rows, late_size, 128)),
+            wide((lanes, late_size, 128)),
         ),
         in_specs=[in_place] * 14,
         out_specs=(in_vmem,) * 4,
@@ -745,9 +742,8 @@
     done = pl.pallas_call(
         format_kernel,
         out_shape=[wide(shape) for shape in shapes],
-        in_specs=[in_place, in_place, in_vmem, in_vmem],
-        out_specs=[in_place, in_place] + [in_vmem] * 12,
-        scratch_shapes=[pltpu.SemaphoreType.DMA((2,))],
+        in_specs=[in_vmem] * 4,
+        out_specs=[in_vmem] * 14,
     )(out, grad, early.reshape(256, 128), late.reshape(128, 128))
     return (
         done[0][None, None],

time: 114 us -> 83.4 us (0.73)
  Pallas kernels: 113 us -> 82.6 us
    pallas_call x1, Pallas kernels: 34.5 us -> 2.38 us  [per_device(): pl.pallas_call(format_kernel, out_shape=[wide(shape) for shape in shapes]...]
    pallas_call x1, Pallas kernels: 78.8 us -> 80.3 us  [per_device(): pl.pallas_call(functools.partial(block_kernel, (rows, lanes), factor, are...]
where the time goes in v2:
time: 83.4 us; the launch traced here: 83.3 us
  Pallas kernels  82.6 us (99%)
    pallas_call x1, Pallas kernels, per_device(): pl.pallas_call(functools.partial(block_kernel, (rows, lanes), factor, are...  80.3 us
    pallas_call x1, Pallas kernels, per_device(): pl.pallas_call(format_kernel, out_shape=[wide(shape) for shape in shapes]...  2.38 us

profile of v2, /device:TPU:1, one launch (start us, length us, event | category | flops | bytes accessed | tf_op | source)
XLA Modules:
  0.0 83.3 jit_solution(6705048861450532525)
XLA Ops:
  0.7 80.3 %shard_map.245 = (f32[64,4,480]{2,1,0:T(4,128)}, f32[64,4,480]{2,1,0:T(4,128)}, f32[16,16,128]{2,1,0:T(8,128)}, f32[16,8,128]{2,1,0:T(8,128)}) custom-call(f32[64,4,480]{2,1,0:T(4,128)} %bitcast.22, f32[64,4,480]{2,1,0:T(4,128)} %bitcast.23, f32[64,128]{1,0:T(8,128)} %bitcast.26, f32[3,3,128]{2,1,0:T(4,128)} %bitcast.30, f32[64,64]{1,0:T(8,128)} %refs_4_.1, ...), custom_call_target="tpu_custom_call" | custom-call | tf_op jit(solution)/shard_map/pallas_call | solution.py:726
  80.9 2.4 %shard_map.246 = (f32[64,4,480]{2,1,0:T(4,128)}, f32[64,4,480]{2,1,0:T(4,128)}, f32[64,128]{1,0:T(8,128)}, f32[3,3,128]{2,1,0:T(4,128)}, f32[64,64]{1,0:T(8,128)...) custom-call(f32[64,4,480]{2,1,0:T(4,128)} %get-tuple-element.32.out_, ...), custom_call_target="tpu_custom_call" | custom-call | tf_op jit(solution)/shard_map/pallas_call | solution.py:742

commit v3 on v2

--- a/solution.py
+++ b/solution.py
@@ -84,9 +84,18 @@
     )
 
 
+def far_first(count, ring):
+    def hops(step):
+        near = step % 8 if ring else step // 4
+        around = 8 if ring else 4
+        return min(near, around - near)
+
+    return sorted(range(1, count), key=lambda step: -hops(step))
+
+
 def block_kernel(sizes, factor, area, cols, *refs):
     operands, results, refs = refs[:14], refs[14:18], refs[18:]
-    out_ref, grad_ref, early_ref, late_ref = results
+    out_hbm, grad_hbm, early_ref, late_ref = results
     (
         x_in, c_in, expand_w, taps_w, pool_w, bias_w, squeeze_w, branch_w,
         up_w, down_w, scale_w, query_w, value_w, cross_w,
@@ -98,7 +107,7 @@
         early, late, early_1, early_2, early_3, late_1, late_2, late_3,
         expand_f, expand_b, squeeze_f, squeeze_b, up_f, up_b, down_f, down_b,
         query_f, query_b, value_f, value_b,
-        loads, sends, recvs, group_sends, group_recvs,
+        out_ref, grad_ref, loads, sends, recvs, group_sends, group_recvs,
     ) = refs[14:]
     rows, lanes = sizes
     row = lax.axis_index("row")
@@ -124,9 +133,9 @@
     partner = {"view": 1 - view}
 
     barrier = pltpu.get_barrier_semaphore()
-    for step in range(1, rows):
+    for step in far_first(rows, True):
         pl.semaphore_signal(barrier, inc=1, device_id=in_row(step), device_id_type=MESH)
-    for step in range(1, lanes):
+    for step in far_first(lanes, False):
         pl.semaphore_signal(barrier, inc=1, device_id=in_lane(step), device_id_type=MESH)
 
     local = [
@@ -160,7 +169,7 @@
                     device_id_type=MESH,
                 )
             )
-            for step in range(1, count)
+            for step in far_first(count, device is in_row)
         ]
 
     def finish(links):
@@ -214,20 +223,7 @@
     for h in range(4):
         c_s[h, :, :cols] = c_in[:, h, :]
 
-    halo_up.wait()
-    halo_down.wait()
-
-    @pl.when(row == 0)
-    def _():
-        x_s[0] = jnp.zeros((64, WIDE), f32)
-
-    @pl.when(row == rows - 1)
-    def _():
-        x_s[5] = jnp.zeros((64, WIDE), f32)
-
     cotangent_sent = send(5, c_s.at[pl.ds(2 - 2 * view, 2)], cp_s, partner)
-    expand_row(0)
-    expand_row(5)
 
     inside = lax.broadcasted_iota(jnp.int32, (1, WIDE), 1) < cols
     fold_s[...] = jnp.zeros_like(fold_s)
@@ -236,8 +232,7 @@
         piece = taps_s[tap, pl.ds(start, size), :]
         return jnp.concatenate([piece] * 4, axis=1)
 
-    @pl.loop(1, 5)
-    def _(h):
+    def conv_row(h):
         for start in range(0, 128, 16):
             columns = [jnp.zeros((16, WIDE), f32)] * 3
             for i in range(3):
@@ -249,6 +244,24 @@
         gate = cv_s[h, :64, :] * cv_s[h, 64:, :]
         g_s[h - 1] = gate
         fold_s[0] += fold(gate)
+
+    pl.loop(2, 4)(conv_row)
+    halo_up.wait()
+    halo_down.wait()
+
+    @pl.when(row == 0)
+    def _():
+        x_s[0] = jnp.zeros((64, WIDE), f32)
+
+    @pl.when(row == rows - 1)
+    def _():
+        x_s[5] = jnp.zeros((64, WIDE), f32)
+
+    expand_row(0)
+    expand_row(5)
+
+    conv_row(1)
+    conv_row(4)
 
     eye = lax.broadcasted_iota(jnp.int32, (64, 128), 0) == lax.broadcasted_iota(
         jnp.int32, (64, 128), 1
@@ -285,8 +298,6 @@
     tap_acc[...] = jnp.zeros_like(tap_acc)
     finish(links)
 
-    conv_up = send(6, cv_s.at[1], cv_s.at[5], above, row != 0, row != rows - 1)
-    conv_down = send(7, cv_s.at[4], cv_s.at[0], below, row != rows - 1, row != 0)
     pooled = jnp.sum(pool_s[...], axis=0) / area
     attention = jnp.sum(pool_w[...] * pooled[:, :64], axis=1, keepdims=True) + bias
 
@@ -307,6 +318,8 @@
     for k in range(2):
         tail_row(theirs[k])
         hidden_sent.append(send(8 + k, h_s.at[theirs[k]], hp_s.at[k], partner))
+    conv_up = send(6, cv_s.at[1], cv_s.at[5], above, row != 0, row != rows - 1)
+    conv_down = send(7, cv_s.at[4], cv_s.at[0], below, row != rows - 1, row != 0)
     for k in range(2):
         tail_row(mine[k])
 
@@ -366,8 +379,6 @@
         other_c = other_c * other_r
         o_s[mine[k]] = own + cross * own_c
         op_s[k] = other + crossp * other_c
-        if k == 0:
-            out_sent.append(send(14, op_s.at[0], o_s.at[mine[0]], partner))
         own_d = cross * own_up * own_r
         other_d = crossp * other_up * other_r
         fold_s[4] += fold(own_up * own_c)
@@ -419,7 +430,6 @@
         )
 
     returned = []
-    out_sent = []
     for k in range(2):
         hidden_sent[k].wait()
         attend_row(k)
@@ -458,7 +468,7 @@
     poolg_s[row, :, :64] = jnp.sum(pool_w[...] * d_attention, axis=0, keepdims=True)
     poolg_s[row, :, 64:] = jnp.zeros((1, 64), f32)
     links = spread(1, lambda step: poolg_s.at[row], poolg_s.at[row], in_row, rows)
-    out_sent.append(send(15, op_s.at[1], o_s.at[mine[1]], partner))
+    out_sent = [send(14 + k, op_s.at[k], o_s.at[mine[k]], partner) for k in range(2)]
 
     query_grads = [jnp.zeros((64, 64), f32)] * 4
     for k in range(2):
@@ -539,11 +549,6 @@
                 columns[1] + pltpu.roll(columns[2], 1, 1) + pltpu.roll(columns[0], WIDE - 1, 1)
             )
 
-    finish(early_links)
-
-    early_2[lane] = jnp.sum(early_1[...], axis=0)
-    early_links = spread(3, lambda step: early_2.at[lane], early_2.at[lane], in_lane, lanes)
-
     late[:64, :] = jnp.zeros((64, 128), f32)
 
     @pl.loop(0, 4)
@@ -575,6 +580,10 @@
         lanes,
     )
     late_1[lane] = late[chunk_at(lane, late_size), :]
+    finish(early_links)
+
+    early_2[lane] = jnp.sum(early_1[...], axis=0)
+    early_links = spread(3, lambda step: early_2.at[lane], early_2.at[lane], in_lane, lanes)
 
     @pl.loop(0, 4)
     def _(h):
@@ -590,17 +599,23 @@
     late_links = spread(6, lambda step: late_2.at[row], late_2.at[row], in_row, rows)
     for h in range(4):
         grad_ref[:, h, :] = dr_s[h, :, :cols]
+    stored = [pltpu.make_async_copy(grad_ref, grad_hbm, loads.at[14])]
+    stored[0].start()
     finish(out_sent)
+    for h in range(4):
+        out_ref[:, h, :] = o_s[h, :, :cols]
+    stored.append(pltpu.make_async_copy(out_ref, out_hbm, loads.at[15]))
+    stored[1].start()
     finish(late_links)
 
     late_3[lane] = jnp.sum(late_2[...], axis=0) * factor
     late_links = spread(7, lambda step: late_3.at[lane], late_3.at[lane], in_lane, lanes)
-    for h in range(4):
-        out_ref[:, h, :] = o_s[h, :, :cols]
     finish(early_links)
     early_ref[...] = early_3[...]
     finish(late_links)
     late_ref[...] = late_3[...]
+    for copy in stored:
+        copy.wait()
 
 
 def format_kernel(out_in, grad_in, early_ref, late_ref, *refs):
@@ -715,7 +730,9 @@
         parts(2, 64, 192),
         parts(2, 64, 192),
         parts(2, 64, 192),
-        pltpu.SemaphoreType.DMA((14,)),
+        fields(64, 4, cols),
+        fields(64, 4, cols),
+        pltpu.SemaphoreType.DMA((16,)),
         pltpu.SemaphoreType.DMA((16,)),
         pltpu.SemaphoreType.DMA((16,)),
         pltpu.SemaphoreType.DMA((8, 15)),
@@ -732,7 +749,7 @@
             wide((lanes, late_size, 128)),
         ),
         in_specs=[in_place] * 14,
-        out_specs=(in_vmem,) * 4,
+        out_specs=(in_place, in_place, in_vmem, in_vmem),
         scratch_shapes=scratch,
         compiler_params=pltpu.CompilerParams(
             collective_id=0, has_side_effects=True, vmem_limit_bytes=56 * 2**20

time: 83.4 us -> 79 us (0.947)
  Pallas kernels: 82.6 us -> 78.2 us
    pallas_call x1, Pallas kernels: 80.3 us -> 75.8 us  [per_device(): pl.pallas_call(functools.partial(block_kernel, (rows, lanes), factor, are...]
where the time goes in v3:
time: 79 us; the launch traced here: 78.8 us
  Pallas kernels  78.2 us (99%)
    pallas_call x1, Pallas kernels, per_device(): pl.pallas_call(functools.partial(block_kernel, (rows, lanes), factor, are...  75.8 us
    pallas_call x1, Pallas kernels, per_device(): pl.pallas_call(format_kernel, out_shape=[wide(shape) for shape in shapes]...  2.38 us

profile of v3, /device:TPU:1, one launch (start us, length us, event | category | flops | bytes accessed | tf_op | source)
XLA Modules:
  0.0 78.8 jit_solution(2158611103195440767)
XLA Ops:
  0.7 75.8 %shard_map.245 = (f32[64,4,480]{2,1,0:T(4,128)}, f32[64,4,480]{2,1,0:T(4,128)}, f32[16,16,128]{2,1,0:T(8,128)}, f32[16,8,128]{2,1,0:T(8,128)}) custom-call(f32[64,4,480]{2,1,0:T(4,128)} %bitcast.22, f32[64,4,480]{2,1,0:T(4,128)} %bitcast.23, f32[64,128]{1,0:T(8,128)} %bitcast.26, f32[3,3,128]{2,1,0:T(4,128)} %bitcast.30, f32[64,64]{1,0:T(8,128)} %refs_4_.1, ...), custom_call_target="tpu_custom_call" | custom-call | tf_op jit(solution)/shard_map/pallas_call | solution.py:743
  76.5 2.4 %shard_map.246 = (f32[64,4,480]{2,1,0:T(4,128)}, f32[64,4,480]{2,1,0:T(4,128)}, f32[64,128]{1,0:T(8,128)}, f32[3,3,128]{2,1,0:T(4,128)}, f32[64,64]{1,0:T(8,128)...) custom-call(f32[64,4,480]{2,1,0:T(4,128)} %get-tuple-element.32.out_, ...), custom_call_target="tpu_custom_call" | custom-call | tf_op jit(solution)/shard_map/pallas_call | solution.py:759

commit v4 on v3

--- a/solution.py
+++ b/solution.py
@@ -103,7 +103,7 @@
     (
         x_s, c_s, cp_s, n0_s, s0_s, d_s, cv_s, g_s, t_s, n1_s, s1_s, e_s, u_s, h_s,
         hp_s, dh_s, dhp_s, o_s, op_s, dg_s, dr_s, de_s, dcv_s, e_att, att_s, attn_s, atts_s,
-        taps_s, fold_s, tap_acc, queryp_s, valuep_s, crossp_s, pool_s, poolg_s,
+        taps_s, fold_s, tap_acc, y_s, w_s, queryp_s, valuep_s, crossp_s, pool_s, poolg_s,
         early, late, early_1, early_2, early_3, late_1, late_2, late_3,
         expand_f, expand_b, squeeze_f, squeeze_b, up_f, up_b, down_f, down_b,
         query_f, query_b, value_f, value_b,
@@ -206,7 +206,7 @@
     @pl.loop(1, 5)
     def _(h):
         value, scale = expand_row(h)
-        n0_s[h - 1] = value
+        n0_s[h] = value
         s0_s[h - 1] = scale
 
     tap_rows = jnp.concatenate(
@@ -257,8 +257,9 @@
     def _():
         x_s[5] = jnp.zeros((64, WIDE), f32)
 
-    expand_row(0)
-    expand_row(5)
+    for h in (0, 5):
+        value, _ = expand_row(h)
+        n0_s[h] = value
 
     conv_row(1)
     conv_row(4)
@@ -296,6 +297,44 @@
     ffn_scale = to_column(scale_w[...])
     cross = to_column(cross_w[...])
     tap_acc[...] = jnp.zeros_like(tap_acc)
+    w_s[...] = jnp.zeros_like(w_s)
+
+    def conv_back(part):
+        @pl.loop(0, 8)
+        def _(chunk):
+            size = 16
+            start = pl.multiple_of(chunk * size, size)
+            for h in range(1, 5):
+                center = dcv_s[h, pl.ds(start, size), :]
+                moved = [pltpu.roll(center, WIDE - 1, 1), center, pltpu.roll(center, 1, 1)]
+                for i in range(3):
+                    value = d_s[h + i - 1, pl.ds(start, size), :]
+                    for j in range(3):
+                        tap_acc[part, 3 * i + j, pl.ds(start, size), :] += fold(moved[j] * value)
+            for h in range(6):
+                columns = [jnp.zeros((size, WIDE), f32)] * 3
+                for i in range(3):
+                    if 1 <= h - i + 1 <= 4:
+                        value = dcv_s[h - i + 1, pl.ds(start, size), :]
+                        for j in range(3):
+                            columns[j] = columns[j] + tap_at(3 * i + j, start, size) * value
+                y_s[part, h, pl.ds(start, size), :] = (
+                    columns[1]
+                    + pltpu.roll(columns[2], 1, 1)
+                    + pltpu.roll(columns[0], WIDE - 1, 1)
+                )
+
+    def expand_products(part):
+        @pl.loop(0, 6)
+        def _(h):
+            w_s[part] += over_pixels(n0_s[h], y_s[part, h])
+
+    @pl.loop(1, 5)
+    def _(h):
+        dcv_s[h, :64, :] = cv_s[h, 64:, :]
+        dcv_s[h, 64:, :] = cv_s[h, :64, :]
+
+    conv_back(0)
     finish(links)
 
     pooled = jnp.sum(pool_s[...], axis=0) / area
@@ -322,6 +361,7 @@
     conv_down = send(7, cv_s.at[4], cv_s.at[0], below, row != rows - 1, row != 0)
     for k in range(2):
         tail_row(mine[k])
+    expand_products(0)
 
     finish(weights_sent)
     query_f[1] = forward_parts(queryp_s[...].T)
@@ -456,20 +496,6 @@
     own_back(1)
     tail_back_row(mine[1])
 
-    returned[0].wait()
-    tail_back_row(theirs[0])
-    gate_theirs = send(
-        13, dg_s.at[theirs[0] + 1], dg_s.at[5 * view], theirs_side, row != other_edge, row != edge
-    )
-    returned[1].wait()
-    tail_back_row(theirs[1])
-
-    d_attention = jnp.sum(fold_s[3], axis=1, keepdims=True)
-    poolg_s[row, :, :64] = jnp.sum(pool_w[...] * d_attention, axis=0, keepdims=True)
-    poolg_s[row, :, 64:] = jnp.zeros((1, 64), f32)
-    links = spread(1, lambda step: poolg_s.at[row], poolg_s.at[row], in_row, rows)
-    out_sent = [send(14 + k, op_s.at[k], o_s.at[mine[k]], partner) for k in range(2)]
-
     query_grads = [jnp.zeros((64, 64), f32)] * 4
     for k in range(2):
         fields = (attn_s[k, 0], attn_s[k, 1], h_s[mine[k]], hp_s[k])
@@ -478,6 +504,22 @@
     for start, pair in ((128, query_grads[:2]), (192, query_grads[2:])):
         early[start : start + 64, :64] = jnp.where(view == 0, pair[0], pair[1])
         early[start : start + 64, 64:] = jnp.where(view == 0, pair[1], pair[0])
+
+    returned[0].wait()
+    tail_back_row(theirs[0])
+    gate_theirs = send(
+        13, dg_s.at[theirs[0] + 1], dg_s.at[5 * view], theirs_side, row != other_edge, row != edge
+    )
+    returned[1].wait()
+    tail_back_row(theirs[1])
+
+    d_attention = jnp.sum(fold_s[3], axis=1, keepdims=True)
+    poolg = jnp.sum(pool_w[...] * d_attention, axis=0, keepdims=True)
+    poolg_s[row, :, :64] = poolg
+    poolg_s[row, :, 64:] = poolg
+    links = spread(1, lambda step: poolg_s.at[row], poolg_s.at[row], in_row, rows)
+    out_sent = [send(14 + k, op_s.at[k], o_s.at[mine[k]], partner) for k in range(2)]
+
     early[:128, :] = jnp.zeros((128, 128), f32)
 
     @pl.loop(0, 4)
@@ -504,64 +546,31 @@
         rows,
     )
     early_1[row] = early[chunk_at(row, early_size), :]
+
+    @pl.loop(1, 5)
+    def _(h):
+        dcv_s[h, :64, :] = dg_s[h] * cv_s[h, 64:, :]
+        dcv_s[h, 64:, :] = dg_s[h] * cv_s[h, :64, :]
+
+    conv_back(1)
+    expand_products(1)
     finish(links)
 
-    constant = to_column(jnp.sum(poolg_s[...], axis=0) / area)
-
-    def gate_back_row(h):
-        total = dg_s[h] + constant
-        dcv_s[h, :64, :] = total * cv_s[h, 64:, :]
-        dcv_s[h, 64:, :] = total * cv_s[h, :64, :]
-
-    pl.loop(1, 5)(gate_back_row)
-    gate_mine.wait()
-    gate_theirs.wait()
-    conv_up.wait()
-    conv_down.wait()
-    for outer, limit in ((0, 0), (5, rows - 1)):
-
-        @pl.when(row == limit)
-        def _():
-            dcv_s[outer] = jnp.zeros((128, WIDE), f32)
-
-        @pl.when(row != limit)
-        def _():
-            gate_back_row(outer)
-
-    @pl.loop(0, 8)
-    def _(chunk):
-        start = pl.multiple_of(chunk * 16, 16)
-        size = 16
-        for h in range(1, 5):
-            center = dcv_s[h, pl.ds(start, size), :]
-            moved = [pltpu.roll(center, WIDE - 1, 1), center, pltpu.roll(center, 1, 1)]
-            for i in range(3):
-                value = d_s[h + i - 1, pl.ds(start, size), :]
-                for j in range(3):
-                    tap_acc[3 * i + j, pl.ds(start, size), :] += fold(moved[j] * value)
-        for h in range(1, 5):
-            columns = [jnp.zeros((size, WIDE), f32)] * 3
-            for i in range(3):
-                value = dcv_s[h - i + 1, pl.ds(start, size), :]
-                for j in range(3):
-                    columns[j] = columns[j] + tap_at(3 * i + j, start, size) * value
-            cv_s[h, pl.ds(start, size), :] = (
-                columns[1] + pltpu.roll(columns[2], 1, 1) + pltpu.roll(columns[0], WIDE - 1, 1)
-            )
-
-    late[:64, :] = jnp.zeros((64, 128), f32)
-
-    @pl.loop(0, 4)
-    def _(h):
-        late[:64, :] += over_pixels(n0_s[h], cv_s[h + 1])
+    constants = jnp.sum(poolg_s[...], axis=0) / area
+    constant = to_column(constants)
+    late[:64, :] = w_s[1] + w_s[0] * constants
 
     place = lax.broadcasted_iota(jnp.int32, (64, 128), 1)
 
     def columns_of(value):
         return jnp.sum(value, axis=1, keepdims=True)
 
-    items = [columns_of(tap_acc[tap, :64, :]) for tap in range(9)]
-    items += [columns_of(tap_acc[tap, 64:, :]) for tap in range(9)]
+    items = [
+        columns_of(tap_acc[1, tap, start : start + 64, :])
+        + constant * columns_of(tap_acc[0, tap, start : start + 64, :])
+        for start in (0, 64)
+        for tap in range(9)
+    ]
     items += [d_attention, columns_of(fold_s[2]), columns_of(fold_s[1])]
     own_cross = columns_of(fold_s[4])
     other_cross = columns_of(fold_s[5])
@@ -585,10 +594,36 @@
     early_2[lane] = jnp.sum(early_1[...], axis=0)
     early_links = spread(3, lambda step: early_2.at[lane], early_2.at[lane], in_lane, lanes)
 
+    gate_mine.wait()
+    gate_theirs.wait()
+    conv_up.wait()
+    conv_down.wait()
+    constant_both = jnp.concatenate([constant, constant], axis=0)
+
+    @pl.loop(1, 5)
+    def _(h):
+        y_s[1, h] += constant_both * y_s[0, h]
+
+    for outer, limit, target, i in ((0, 0, 1, 2), (5, rows - 1, 4, 0)):
+
+        @pl.when(row != limit)
+        def _():
+            total = dg_s[outer] + constant
+            dcv_s[outer, :64, :] = total * cv_s[outer, 64:, :]
+            dcv_s[outer, 64:, :] = total * cv_s[outer, :64, :]
+            for start in range(0, 128, 16):
+                value = dcv_s[outer, start : start + 16, :]
+                columns = [tap_at(3 * i + j, start, 16) * value for j in range(3)]
+                y_s[1, target, start : start + 16, :] += (
+                    columns[1]
+                    + pltpu.roll(columns[2], 1, 1)
+                    + pltpu.roll(columns[0], WIDE - 1, 1)
+                )
+
     @pl.loop(0, 4)
     def _(h):
-        dn = dot_nn(expand_b[...], right_parts(cv_s[h + 1]))
-        dr_s[h] = dr_s[h] + normed_back(dn, n0_s[h], s0_s[h])
+        dn = dot_nn(expand_b[...], right_parts(y_s[1, h + 1]))
+        dr_s[h] = dr_s[h] + normed_back(dn, n0_s[h + 1], s0_s[h])
 
     finish(early_links)
     early_3[row] = jnp.sum(early_2[...], axis=0) * factor
@@ -678,7 +713,7 @@
         fields(6, 64, WIDE),
         fields(4, 64, WIDE),
         fields(2, 64, WIDE),
-        fields(4, 64, WIDE),
+        fields(6, 64, WIDE),
         fields(4, 1, WIDE),
         fields(6, 128, WIDE),
         fields(6, 128, WIDE),
@@ -704,7 +739,9 @@
         fields(2, 1, WIDE),
         fields(9, 128, 128),
         fields(6, 64, 128),
-        fields(9, 128, 128),
+        fields(2, 9, 128, 128),
+        fields(2, 6, 128, WIDE),
+        fields(2, 64, 128),
         fields(64, 64),
         fields(64, 64),
         fields(1, 64),

time: 79 us -> 78 us (0.987)
  Pallas kernels: 78.2 us -> 77.2 us
    pallas_call x1, Pallas kernels: 75.8 us -> 74.8 us  [per_device(): pl.pallas_call(functools.partial(block_kernel, (rows, lanes), factor, are...]
where the time goes in v4:
time: 78 us; the launch traced here: 77.9 us
  Pallas kernels  77.2 us (99%)
    pallas_call x1, Pallas kernels, per_device(): pl.pallas_call(functools.partial(block_kernel, (rows, lanes), factor, are...  74.8 us
    pallas_call x1, Pallas kernels, per_device(): pl.pallas_call(format_kernel, out_shape=[wide(shape) for shape in shapes]...  2.38 us

profile of v4, /device:TPU:1, one launch (start us, length us, event | category | flops | bytes accessed | tf_op | source)
XLA Modules:
  0.0 77.9 jit_solution(4277972684810393477)
XLA Ops:
  0.7 74.8 %shard_map.245 = (f32[64,4,480]{2,1,0:T(4,128)}, f32[64,4,480]{2,1,0:T(4,128)}, f32[16,16,128]{2,1,0:T(8,128)}, f32[16,8,128]{2,1,0:T(8,128)}) custom-call(f32[64,4,480]{2,1,0:T(4,128)} %bitcast.22, f32[64,4,480]{2,1,0:T(4,128)} %bitcast.23, f32[64,128]{1,0:T(8,128)} %bitcast.26, f32[3,3,128]{2,1,0:T(4,128)} %bitcast.30, f32[64,64]{1,0:T(8,128)} %refs_4_.1, ...), custom_call_target="tpu_custom_call" | custom-call | tf_op jit(solution)/shard_map/pallas_call | solution.py:780
  75.5 2.4 %shard_map.246 = (f32[64,4,480]{2,1,0:T(4,128)}, f32[64,4,480]{2,1,0:T(4,128)}, f32[64,128]{1,0:T(8,128)}, f32[3,3,128]{2,1,0:T(4,128)}, f32[64,64]{1,0:T(8,128)...) custom-call(f32[64,4,480]{2,1,0:T(4,128)} %get-tuple-element.32.out_, ...), custom_call_target="tpu_custom_call" | custom-call | tf_op jit(solution)/shard_map/pallas_call | solution.py:796

commit v5 on v4

--- a/solution.py
+++ b/solution.py
@@ -102,7 +102,7 @@
     ) = refs[:14]
     (
         x_s, c_s, cp_s, n0_s, s0_s, d_s, cv_s, g_s, t_s, n1_s, s1_s, e_s, u_s, h_s,
-        hp_s, dh_s, dhp_s, o_s, op_s, dg_s, dr_s, de_s, dcv_s, e_att, att_s, attn_s, atts_s,
+        hp_s, dh_s, dhp_s, o_s, op_s, dg_s, dr_s, de_s, dcv_s, e_att, att_s, attn_s, atts_s, own_s,
         taps_s, fold_s, tap_acc, y_s, w_s, queryp_s, valuep_s, crossp_s, pool_s, poolg_s,
         early, late, early_1, early_2, early_3, late_1, late_2, late_3,
         expand_f, expand_b, squeeze_f, squeeze_b, up_f, up_b, down_f, down_b,
@@ -381,17 +381,21 @@
         sixteen == 0, 1.0, jnp.where((sixteen == 1) & outside16, -256.0, 0.0)
     ).astype(bf16)
 
+    def own_parts(k):
+        own = h_s[mine[k]]
+        own_n, own_scale = normed(own)
+        attn_s[k, 0] = own_n
+        atts_s[k] = own_scale
+        own_s[k, 0] = dot_nn(query_f[0], right_parts(own_n))
+        own_s[k, 1] = dot_nn(value_f[0], right_parts(own))
+
     def attend_row(k):
         own, other = h_s[mine[k]], hp_s[k]
         own_up, other_up = c_s[mine[k]], cp_s[slots[k]]
-        own_n, own_scale = normed(own)
         other_n, other_scale = normed(other)
-        attn_s[k, 0] = own_n
         attn_s[k, 1] = other_n
-        atts_s[k] = own_scale
-        own_q = dot_nn(query_f[0], right_parts(own_n))
+        own_q, own_v = own_s[k, 0], own_s[k, 1]
         other_q = dot_nn(query_f[1], right_parts(other_n))
-        own_v = dot_nn(value_f[0], right_parts(own))
         other_v = dot_nn(value_f[1], right_parts(other))
         scores = dot_tn(
             jnp.concatenate([left_parts(own_q * 0.125), mask_left], axis=0),
@@ -417,12 +421,8 @@
         other_c, other_r = weighted(dot_nn, own_v)
         own_c = own_c * own_r
         other_c = other_c * other_r
-        o_s[mine[k]] = own + cross * own_c
-        op_s[k] = other + crossp * other_c
         own_d = cross * own_up * own_r
         other_d = crossp * other_up * other_r
-        fold_s[4] += fold(own_up * own_c)
-        fold_s[5] += fold(other_up * other_c)
         own_delta, own_delta_low = halves(-jnp.sum(own_d * own_c, axis=0, keepdims=True))
         other_delta, other_delta_low = halves(-jnp.sum(other_d * other_c, axis=0, keepdims=True))
         left_tail = jnp.where(
@@ -456,6 +456,11 @@
             + dot_nn(value_b[1], right_parts(other_dv))
             + normed_back(dn, other_n, other_scale)
         )
+        returned.append(send(10 + k, dhp_s.at[k], dh_s.at[mine[k]], partner))
+        o_s[mine[k]] = own + cross * own_c
+        op_s[k] = other + crossp * other_c
+        fold_s[4] += fold(own_up * own_c)
+        fold_s[5] += fold(other_up * other_c)
         att_s[k, 1] = other_dq
         att_s[k, 3] = other_dv
         att_s[k, 2] = through(dot_nt, other_d, w_high, w_low)
@@ -471,9 +476,10 @@
 
     returned = []
     for k in range(2):
+        own_parts(k)
+    for k in range(2):
         hidden_sent[k].wait()
         attend_row(k)
-        returned.append(send(10 + k, dhp_s.at[k], dh_s.at[mine[k]], partner))
 
     def tail_back_row(h):
         up = dh_s[h]
@@ -533,19 +539,19 @@
         early[64:128, :64] += over_pixels(branch * dr, g_s[h] * attention)
         early[64:128, 64:] += over_pixels(ffn_scale * up, expanded[:64] * expanded[64:])
 
-    early_size, late_size = 256 // rows, 128 // lanes
+    early_size, late_size = 256 // lanes, 128 // lanes
 
     def chunk_at(index, size):
         return pl.ds(pl.multiple_of(index * size, 8), size)
 
     early_links = spread(
         2,
-        lambda step: early.at[chunk_at(lax.rem(row + step, rows), early_size)],
-        early_1.at[row],
-        in_row,
-        rows,
-    )
-    early_1[row] = early[chunk_at(row, early_size), :]
+        lambda step: early.at[chunk_at(lax.rem(lane + step, lanes), early_size)],
+        early_1.at[lane],
+        in_lane,
+        lanes,
+    )
+    early_1[lane] = early[chunk_at(lane, early_size), :]
 
     @pl.loop(1, 5)
     def _(h):
@@ -581,6 +587,7 @@
         mixed = jnp.where(place == 64 + index, item, mixed)
     late[64:, :] = mixed
 
+    constant_both = jnp.concatenate([constant, constant], axis=0)
     late_links = spread(
         5,
         lambda step: late.at[chunk_at(lax.rem(lane + step, lanes), late_size)],
@@ -589,21 +596,23 @@
         lanes,
     )
     late_1[lane] = late[chunk_at(lane, late_size), :]
+
+    @pl.loop(1, 5)
+    def _(h):
+        y_s[1, h] += constant_both * y_s[0, h]
+
+    finish(late_links)
+
+    late_2[row] = jnp.sum(late_1[...], axis=0)
+    late_links = spread(6, lambda step: late_2.at[row], late_2.at[row], in_row, rows)
     finish(early_links)
-
-    early_2[lane] = jnp.sum(early_1[...], axis=0)
-    early_links = spread(3, lambda step: early_2.at[lane], early_2.at[lane], in_lane, lanes)
+    early_2[row] = jnp.sum(early_1[...], axis=0)
+    early_links = spread(3, lambda step: early_2.at[row], early_2.at[row], in_row, rows)
 
     gate_mine.wait()
     gate_theirs.wait()
     conv_up.wait()
     conv_down.wait()
-    constant_both = jnp.concatenate([constant, constant], axis=0)
-
-    @pl.loop(1, 5)
-    def _(h):
-        y_s[1, h] += constant_both * y_s[0, h]
-
     for outer, limit, target, i in ((0, 0, 1, 2), (5, rows - 1, 4, 0)):
 
         @pl.when(row != limit)
@@ -625,26 +634,22 @@
         dn = dot_nn(expand_b[...], right_parts(y_s[1, h + 1]))
         dr_s[h] = dr_s[h] + normed_back(dn, n0_s[h + 1], s0_s[h])
 
-    finish(early_links)
-    early_3[row] = jnp.sum(early_2[...], axis=0) * factor
-    early_links = spread(4, lambda step: early_3.at[row], early_3.at[row], in_row, rows)
-    finish(late_links)
-
-    late_2[row] = jnp.sum(late_1[...], axis=0)
-    late_links = spread(6, lambda step: late_2.at[row], late_2.at[row], in_row, rows)
     for h in range(4):
         grad_ref[:, h, :] = dr_s[h, :, :cols]
     stored = [pltpu.make_async_copy(grad_ref, grad_hbm, loads.at[14])]
     stored[0].start()
+    finish(late_links)
+
+    late_3[lane] = jnp.sum(late_2[...], axis=0) * factor
+    late_links = spread(7, lambda step: late_3.at[lane], late_3.at[lane], in_lane, lanes)
+    finish(early_links)
+    early_3[lane] = jnp.sum(early_2[...], axis=0) * factor
+    early_links = spread(4, lambda step: early_3.at[lane], early_3.at[lane], in_lane, lanes)
     finish(out_sent)
     for h in range(4):
         out_ref[:, h, :] = o_s[h, :, :cols]
     stored.append(pltpu.make_async_copy(out_ref, out_hbm, loads.at[15]))
     stored[1].start()
-    finish(late_links)
-
-    late_3[lane] = jnp.sum(late_2[...], axis=0) * factor
-    late_links = spread(7, lambda step: late_3.at[lane], late_3.at[lane], in_lane, lanes)
     finish(early_links)
     early_ref[...] = early_3[...]
     finish(late_links)
@@ -708,7 +713,7 @@
         arrays[12][0],
         arrays[13],
     ]
-    early_size, late_size = 256 // rows, 128 // lanes
+    early_size, late_size = 256 // lanes, 128 // lanes
     scratch = [fields(*operand.shape) for operand in operands] + [
         fields(6, 64, WIDE),
         fields(4, 64, WIDE),
@@ -737,6 +742,7 @@
         fields(2, 4, 64, WIDE),
         fields(2, 2, 64, WIDE),
         fields(2, 1, WIDE),
+        fields(2, 2, 64, WIDE),
         fields(9, 128, 128),
         fields(6, 64, 128),
         fields(2, 9, 128, 128),
@@ -749,9 +755,9 @@
         fields(rows, 1, 128),
         fields(256, 128),
         fields(128, 128),
+        fields(lanes, early_size, 128),
         fields(rows, early_size, 128),
         fields(lanes, early_size, 128),
-        fields(rows, early_size, 128),
         fields(lanes, late_size, 128),
         fields(rows, late_size, 128),
         fields(lanes, late_size, 128),
@@ -782,7 +788,7 @@
         out_shape=(
             wide((64, 4, cols)),
             wide((64, 4, cols)),
-            wide((rows, early_size, 128)),
+            wide((lanes, early_size, 128)),
             wide((lanes, late_size, 128)),
         ),
         in_specs=[in_place] * 14,

time: 78 us -> 73.2 us (0.938)
  Pallas kernels: 77.2 us -> 72.4 us
    pallas_call x1, Pallas kernels: 74.8 us -> 70 us  [per_device(): pl.pallas_call(functools.partial(block_kernel, (rows, lanes), factor, are...]
where the time goes in v5:
time: 73.2 us; the launch traced here: 73 us
  Pallas kernels  72.4 us (99%)
    pallas_call x1, Pallas kernels, per_device(): pl.pallas_call(functools.partial(block_kernel, (rows, lanes), factor, are...  70 us
    pallas_call x1, Pallas kernels, per_device(): pl.pallas_call(format_kernel, out_shape=[wide(shape) for shape in shapes]...  2.38 us

profile of v5, /device:TPU:1, one launch (start us, length us, event | category | flops | bytes accessed | tf_op | source)
XLA Modules:
  0.0 73.0 jit_solution(2129140133144827609)
XLA Ops:
  0.7 70.0 %shard_map.245 = (f32[64,4,480]{2,1,0:T(4,128)}, f32[64,4,480]{2,1,0:T(4,128)}, f32[16,16,128]{2,1,0:T(8,128)}, f32[16,8,128]{2,1,0:T(8,128)}) custom-call(f32[64,4,480]{2,1,0:T(4,128)} %bitcast.22, f32[64,4,480]{2,1,0:T(4,128)} %bitcast.23, f32[64,128]{1,0:T(8,128)} %bitcast.26, f32[3,3,128]{2,1,0:T(4,128)} %bitcast.30, f32[64,64]{1,0:T(8,128)} %refs_4_.1, ...), custom_call_target="tpu_custom_call" | custom-call | tf_op jit(solution)/shard_map/pallas_call | solution.py:786
  70.7 2.4 %shard_map.246 = (f32[64,4,480]{2,1,0:T(4,128)}, f32[64,4,480]{2,1,0:T(4,128)}, f32[64,128]{1,0:T(8,128)}, f32[3,3,128]{2,1,0:T(4,128)}, f32[64,64]{1,0:T(8,128)...) custom-call(f32[64,4,480]{2,1,0:T(4,128)} %get-tuple-element.32.out_, ...), custom_call_target="tpu_custom_call" | custom-call | tf_op jit(solution)/shard_map/pallas_call | solution.py:802

commit v6 on v5

--- a/solution.py
+++ b/solution.py
@@ -524,7 +524,6 @@
     poolg_s[row, :, :64] = poolg
     poolg_s[row, :, 64:] = poolg
     links = spread(1, lambda step: poolg_s.at[row], poolg_s.at[row], in_row, rows)
-    out_sent = [send(14 + k, op_s.at[k], o_s.at[mine[k]], partner) for k in range(2)]
 
     early[:128, :] = jnp.zeros((128, 128), f32)
 
@@ -595,6 +594,7 @@
         in_lane,
         lanes,
     )
+    out_sent = [send(14 + k, op_s.at[k], o_s.at[mine[k]], partner) for k in range(2)]
     late_1[lane] = late[chunk_at(lane, late_size), :]
 
     @pl.loop(1, 5)

time: 73.2 us -> 73.1 us (level)
  no operation moved by 1% of the time
where the time goes in v6:
time: 73.1 us; the launch traced here: 73 us
  Pallas kernels  72.3 us (99%)
    pallas_call x1, Pallas kernels, per_device(): pl.pallas_call(functools.partial(block_kernel, (rows, lanes), factor, are...  69.9 us
    pallas_call x1, Pallas kernels, per_device(): pl.pallas_call(format_kernel, out_shape=[wide(shape) for shape in shapes]...  2.38 us

profile of v6, /device:TPU:1, one launch (start us, length us, event | category | flops | bytes accessed | tf_op | source)
XLA Modules:
  0.0 73.0 jit_solution(3420009783881710017)
XLA Ops:
  0.7 69.9 %shard_map.245 = (f32[64,4,480]{2,1,0:T(4,128)}, f32[64,4,480]{2,1,0:T(4,128)}, f32[16,16,128]{2,1,0:T(8,128)}, f32[16,8,128]{2,1,0:T(8,128)}) custom-call(f32[64,4,480]{2,1,0:T(4,128)} %bitcast.22, f32[64,4,480]{2,1,0:T(4,128)} %bitcast.23, f32[64,128]{1,0:T(8,128)} %bitcast.26, f32[3,3,128]{2,1,0:T(4,128)} %bitcast.30, f32[64,64]{1,0:T(8,128)} %refs_4_.1, ...), custom_call_target="tpu_custom_call" | custom-call | tf_op jit(solution)/shard_map/pallas_call | solution.py:786
  70.6 2.4 %shard_map.246 = (f32[64,4,480]{2,1,0:T(4,128)}, f32[64,4,480]{2,1,0:T(4,128)}, f32[64,128]{1,0:T(8,128)}, f32[3,3,128]{2,1,0:T(4,128)}, f32[64,64]{1,0:T(8,128)...) custom-call(f32[64,4,480]{2,1,0:T(4,128)} %get-tuple-element.32.out_, ...), custom_call_target="tpu_custom_call" | custom-call | tf_op jit(solution)/shard_map/pallas_call | solution.py:802
